TPU v7x, 512 devices: a whole 4x4x16 slice. The times are simulated.
512 devices in a mesh: leaf: 64 (over z, y), oct: 8 (over x, core).
Axes of the slice: x: 4, y: 4, z: 16, core: 2. Of those that a mesh axis runs over, the one named last changes fastest.
Arguments:
- children: bfloat16 [16384, 4096], P(('leaf', 'oct')), may hold values from -6 to 6
- child_slot: int32 [2048, 8], P('leaf', 'oct'), may hold values from 0 to 31, as said below
- two_scale: bfloat16 [32, 32], replicated, may hold values from -1 to 1
- factors: bfloat16 [27, 30720], replicated, may hold values from -0.5390625 to 0.5390625
- disp_kind: int32 [2048, 4], P(('leaf', 'oct')), may hold values from 0 to 26
- target_leaf: int32 [2048, 4, 1], P(('leaf', 'oct')), may hold values from 0 to 63; in each aligned block of 16 rows (0 to 15, 16 to 31, ..., all dimensions but the last counted through in order) at most 2 rows name the same one
- target_node: int32 [2048, 4], P(('leaf', 'oct')), may hold values from 0 to 15
Outputs:
- octant_out: bfloat16 [1024, 8, 4096], P('leaf', 'oct')
Inputs may be any that keep to these rules, and one draw needn't show every extreme that they name: Over the parents of one subtree and the octants held by one device along oct, child_slot takes every value exactly once. `target_leaf`: of the 16 entries of one device, at most 2 name the same subtree; some device reaches 2.
All inputs are finite; a program needn't handle non-finite values.
Results may differ from a plain program's by a relative error of at most 0.018.
Values may be sent and summed in bfloat16 or wider, within the bound.
A program may use at most 64 MiB of HBM per device.

v0:
```python
import jax
import jax.numpy as jnp
from jax import lax
from jax.sharding import PartitionSpec as P

TGT_DEV = 2


def filter_blocks(block_batch, filter_halfset):
    half_edge = filter_halfset.shape[2]
    count_batch = block_batch.shape[0]
    split_blocks = block_batch.reshape(count_batch, 2, 2, 2, half_edge, half_edge, half_edge)
    first_pass = jnp.einsum(
        "nijlpsr,aip->najlsr", split_blocks, filter_halfset, preferred_element_type=jnp.float32
    ).astype(jnp.bfloat16)
    second_sweep = jnp.einsum(
        "najlsr,bjs->nablr", first_pass, filter_halfset, preferred_element_type=jnp.float32
    ).astype(jnp.bfloat16)
    return jnp.einsum(
        "qyixz,wxz->qyiw", second_sweep, filter_halfset, preferred_element_type=jnp.float32
    ).astype(jnp.bfloat16)


def unfilter_blocks(cube_batch, filter_halfset):
    half_edge = filter_halfset.shape[2]
    count_batch = cube_batch.shape[0]
    first_pass = jnp.einsum(
        "nabc,aip->nipbc", cube_batch, filter_halfset, preferred_element_type=jnp.float32
    ).astype(jnp.bfloat16)
    second_sweep = jnp.einsum(
        "nipbc,bjs->nipjsc", first_pass, filter_halfset, preferred_element_type=jnp.float32
    ).astype(jnp.bfloat16)
    third_sweep = jnp.einsum(
        "xmezhw,wbf->xmezhbf", second_sweep, filter_halfset, preferred_element_type=jnp.float32
    ).astype(jnp.bfloat16)
    ordered = jnp.transpose(third_sweep, (0, 1, 3, 5, 2, 4, 6))
    return ordered.reshape(count_batch, 8, half_edge * half_edge * half_edge)


def apply_parent(parent_item):
    parent_cube, factor_rows = parent_item
    edge_len = parent_cube.shape[0]
    factor_set = factor_rows.reshape(factor_rows.shape[0], 3, -1, edge_len, edge_len)
    section_z = jnp.einsum(
        "abc,ktdc->ktabd", parent_cube, factor_set[:, 2], preferred_element_type=jnp.float32
    ).astype(jnp.bfloat16)
    section_y = jnp.einsum(
        "ktabd,kteb->ktaed", section_z, factor_set[:, 1], preferred_element_type=jnp.float32
    ).astype(jnp.bfloat16)
    summed = jnp.einsum(
        "ktaed,ktfa->kfed", section_y, factor_set[:, 0], preferred_element_type=jnp.float32
    ).astype(jnp.bfloat16)
    return summed.reshape(summed.shape[0], -1)


def local(children, child_slot, two_scale, factors, disp_kind, target_leaf, target_node):
    oct_count = lax.axis_size("oct")
    leaf_count = lax.axis_size("leaf")
    edge_len = two_scale.shape[0]
    half_edge = edge_len // 2
    cube_len = edge_len * edge_len * edge_len
    filter_halfset = two_scale.reshape(edge_len, 2, half_edge)
    picked_blocks = children[child_slot]
    octant_blocks = lax.all_to_all(picked_blocks, "oct", split_axis=0, concat_axis=1, tiled=True)
    parent_blocks = filter_blocks(octant_blocks, filter_halfset)
    kind_factors = factors[disp_kind]
    contributions = lax.map(apply_parent, (parent_blocks, kind_factors))
    flat_rows = contributions.reshape(-1, cube_len)
    row_total = flat_rows.shape[0]
    leaf_numbers = target_leaf.reshape(-1)
    node_numbers = target_node.reshape(-1)
    slot_count = max(2, (2 * row_total + leaf_count - 1) // leaf_count)
    row_order = jnp.arange(row_total, dtype=jnp.int32)
    earlier_same = (leaf_numbers[:, None] == leaf_numbers[None, :]) & (
        row_order[None, :] < row_order[:, None]
    )
    slot_rank = jnp.sum(earlier_same.astype(jnp.int32), axis=1)
    slot_index = leaf_numbers * slot_count + slot_rank
    slot_chooser = (
        jnp.arange(leaf_count * slot_count, dtype=jnp.int32)[:, None] == slot_index[None, :]
    )
    packed_rows = jnp.dot(
        slot_chooser.astype(jnp.bfloat16), flat_rows, preferred_element_type=jnp.float32
    ).astype(jnp.bfloat16)
    packed_ids = jnp.sum(jnp.where(slot_chooser, node_numbers[None, :] + 1, 0), axis=1) - 1
    arrived, arrived_ids = (
        lax.all_to_all(
            packed_rows.reshape(leaf_count, slot_count, cube_len),
            "leaf",
            split_axis=0,
            concat_axis=0,
            tiled=True,
        ),
        lax.all_to_all(
            packed_ids.reshape(leaf_count, slot_count),
            "leaf",
            split_axis=0,
            concat_axis=0,
            tiled=True,
        ),
    )
    node_count = TGT_DEV * oct_count
    node_select = (
        jnp.arange(node_count, dtype=jnp.int32)[:, None] == arrived_ids.reshape(-1)[None, :]
    ).astype(jnp.bfloat16)
    partial_totals = jnp.dot(
        node_select, arrived.reshape(-1, cube_len), preferred_element_type=jnp.float32
    )
    held_octants = 8 // oct_count
    node_totals = lax.psum(partial_totals.astype(jnp.bfloat16), "oct")
    child_blocks = unfilter_blocks(
        node_totals.reshape(node_count, edge_len, edge_len, edge_len), filter_halfset
    )
    return lax.dynamic_slice_in_dim(
        child_blocks, lax.axis_index("oct") * held_octants, held_octants, 1
    )


def solution(mesh):
    placed = (
        P(("leaf", "oct"), None),
        P("leaf", "oct"),
        P(),
        P(),
        P(("leaf", "oct"), None),
        P(("leaf", "oct"), None, None),
        P(("leaf", "oct"), None),
    )
    return jax.shard_map(
        local, mesh=mesh, in_specs=placed, out_specs=P("leaf", "oct", None), check_vma=False
    )
```

profile of v0, /device:TPU:8, one launch (start us, length us, event | category | flops | bytes accessed | tf_op | source)
XLA Modules:
  0.0 762.0 jit_solution(11017069444148070624)
XLA Ops:
  11.5 4.3 all-to-all-start.1
  23.5 18.7 %all-to-all-start = ((s32[64,1,2]{2,1,0:T(1,128)}), s32[64,1,2]{2,1,0:T(1,128)S(1)}, u32[]{:S(2)}, u32[]{:S(2)}) async-start(s32[64,1,2]{2,1,0:T(1,128)} %bitcast.16), calls=%async_computation | async-start | bytes 65536 | tf_op jit(solution)/shard_map/all_to_all | solution.py:94
  56.4 134.9 %while.10 = (s32[]{:T(128)}, bf16[4,4,32768]{2,1,0:T(4,128)(2,1)}, bf16[4,4,30720]{2,1,0:T(4,128)(2,1)}, bf16[4,32,32,32]{3,2,1,0:T(8,128)(2,1)S(1)}, s32[]{:T(128)}) while((s32[]{:T(128)}, bf16[4,4,32768]{2,1,0:T(4,128)(2,1)}, bf16[4,4,30720]{2,1,0:T(4,128)(2,1)}, bf16[4,32,32,32]{3,2,1,0:T(8,128)(2,1)S(1)}, s32[]{:T(128)}) %tuple.18), condition=%wide.region_3.4_spmd, body=%wide.region_2.3_spmd.sunk | while | flops 254410752 | bytes 9306193 | solution.py:67
  58.2 21.0 %convert_bitcast_fusion.4 = bf16[4,10,32,32,32]{4,3,2,1,0:T(8,128)(2,1)} fusion(bf16[4,3,10,32,32]{4,3,2,1,0:T(8,128)(2,1)S(1)} %reshape.130, bf16[4,32,32,32]{3,2,1,0:T(8,128)(2,1)S(1)} %get-tuple-element.74, s32[]{:T(128)S(6)} %copy.108), kind=kOutput, calls=%fused_computation.6.clone.1 | convolution fusion | flops 170393600 | bytes 3538948 | tf_op jit(solution)/shard_map/while/body/eval_jaxpr/ktabd,kteb->ktaed/dot_general | solution.py:47
  79.2 8.8 %bitcast_convert_fusion.5 = bf16[4,32,32,32]{3,1,2,0:T(8,128)(2,1)S(1)} fusion(bf16[4,10,32,32,32]{4,3,2,1,0:T(8,128)(2,1)} %convert_bitcast_fusion.4, bf16[4,3,10,32,32]{4,3,2,1,0:T(8,128)(2,1)S(1)} %reshape.130), kind=kOutput, calls=%fused_computation.9.clone.1 | convolution fusion | flops 84017152 | bytes 3211264 | tf_op jit(solution)/shard_map/while/body/eval_jaxpr/ktaed,ktfa->kfed/dot_general | solution.py:50
  91.9 21.0 %convert_bitcast_fusion.4 = bf16[4,10,32,32,32]{4,3,2,1,0:T(8,128)(2,1)} fusion(bf16[4,3,10,32,32]{4,3,2,1,0:T(8,128)(2,1)S(1)} %reshape.130, bf16[4,32,32,32]{3,2,1,0:T(8,128)(2,1)S(1)} %get-tuple-element.74, s32[]{:T(128)S(6)} %copy.108), kind=kOutput, calls=%fused_computation.6.clone.1 | convolution fusion | flops 170393600 | bytes 3538948 | tf_op jit(solution)/shard_map/while/body/eval_jaxpr/ktabd,kteb->ktaed/dot_general | solution.py:47
  112.9 8.8 %bitcast_convert_fusion.5 = bf16[4,32,32,32]{3,1,2,0:T(8,128)(2,1)S(1)} fusion(bf16[4,10,32,32,32]{4,3,2,1,0:T(8,128)(2,1)} %convert_bitcast_fusion.4, bf16[4,3,10,32,32]{4,3,2,1,0:T(8,128)(2,1)S(1)} %reshape.130), kind=kOutput, calls=%fused_computation.9.clone.1 | convolution fusion | flops 84017152 | bytes 3211264 | tf_op jit(solution)/shard_map/while/body/eval_jaxpr/ktaed,ktfa->kfed/dot_general | solution.py:50
  125.6 21.0 %convert_bitcast_fusion.4 = bf16[4,10,32,32,32]{4,3,2,1,0:T(8,128)(2,1)} fusion(bf16[4,3,10,32,32]{4,3,2,1,0:T(8,128)(2,1)S(1)} %reshape.130, bf16[4,32,32,32]{3,2,1,0:T(8,128)(2,1)S(1)} %get-tuple-element.74, s32[]{:T(128)S(6)} %copy.108), kind=kOutput, calls=%fused_computation.6.clone.1 | convolution fusion | flops 170393600 | bytes 3538948 | tf_op jit(solution)/shard_map/while/body/eval_jaxpr/ktabd,kteb->ktaed/dot_general | solution.py:47
  146.6 8.8 %bitcast_convert_fusion.5 = bf16[4,32,32,32]{3,1,2,0:T(8,128)(2,1)S(1)} fusion(bf16[4,10,32,32,32]{4,3,2,1,0:T(8,128)(2,1)} %convert_bitcast_fusion.4, bf16[4,3,10,32,32]{4,3,2,1,0:T(8,128)(2,1)S(1)} %reshape.130), kind=kOutput, calls=%fused_computation.9.clone.1 | convolution fusion | flops 84017152 | bytes 3211264 | tf_op jit(solution)/shard_map/while/body/eval_jaxpr/ktaed,ktfa->kfed/dot_general | solution.py:50
  159.3 21.0 %convert_bitcast_fusion.4 = bf16[4,10,32,32,32]{4,3,2,1,0:T(8,128)(2,1)} fusion(bf16[4,3,10,32,32]{4,3,2,1,0:T(8,128)(2,1)S(1)} %reshape.130, bf16[4,32,32,32]{3,2,1,0:T(8,128)(2,1)S(1)} %get-tuple-element.74, s32[]{:T(128)S(6)} %copy.108), kind=kOutput, calls=%fused_computation.6.clone.1 | convolution fusion | flops 170393600 | bytes 3538948 | tf_op jit(solution)/shard_map/while/body/eval_jaxpr/ktabd,kteb->ktaed/dot_general | solution.py:47
  180.3 8.8 %bitcast_convert_fusion.5 = bf16[4,32,32,32]{3,1,2,0:T(8,128)(2,1)S(1)} fusion(bf16[4,10,32,32,32]{4,3,2,1,0:T(8,128)(2,1)} %convert_bitcast_fusion.4, bf16[4,3,10,32,32]{4,3,2,1,0:T(8,128)(2,1)S(1)} %reshape.130), kind=kOutput, calls=%fused_computation.9.clone.1 | convolution fusion | flops 84017152 | bytes 3211264 | tf_op jit(solution)/shard_map/while/body/eval_jaxpr/ktaed,ktfa->kfed/dot_general | solution.py:50
  192.7 5.7 convolution_convert_fusion
  198.4 14.1 %reshape.72 = bf16[64,2,32768]{2,1,0:T(2,128)(2,1)} reshape(bf16[128,32768]{1,0:T(8,128)(2,1)} %convolution_convert_fusion) | data formatting | bytes 16777216 | tf_op jit(solution)/shard_map/reshape | solution.py:88
  212.5 15.3 %all-to-all-start.2 = ((bf16[64,2,32768]{2,1,0:T(2,128)(2,1)}), bf16[64,2,32768]{2,1,0:T(2,128)(2,1)}, u32[]{:S(2)}, u32[]{:S(2)}) async-start(bf16[64,2,32768]{2,1,0:T(2,128)(2,1)} %reshape.72), calls=%async_computation.2 | async-start | bytes 16777216 | tf_op jit(solution)/shard_map/all_to_all | solution.py:87
  228.6 369.0 %all-to-all-done.2 = bf16[64,2,32768]{2,1,0:T(2,128)(2,1)} async-done(((bf16[64,2,32768]{2,1,0:T(2,128)(2,1)}), bf16[64,2,32768]{2,1,0:T(2,128)(2,1)}, u32[]{:S(2)}, u32[]{:S(2)}) %all-to-all-start.2) | async-done | bytes 8388640 | tf_op jit(solution)/shard_map/all_to_all | solution.py:87
  597.6 22.7 %reshape.73 = bf16[128,32768]{1,0:T(8,128)(2,1)} reshape(bf16[64,2,32768]{2,1,0:T(2,128)(2,1)} %all-to-all-done.2) | data formatting | bytes 16777216 | tf_op jit(solution)/shard_map/reshape | solution.py:107
  620.3 4.6 convolution_convert_fusion.1
  624.9 4.6 reshape.74
  629.5 5.9 copy.57
  635.4 79.6 %all-reduce.2.cloned.1.call-done = bf16[16,32,32,32]{3,1,2,0:T(8,128)(2,1)} async-done(((bf16[16,32,32,32]{3,1,2,0:T(8,128)(2,1)}), bf16[16,32,32,32]{3,1,2,0:T(8,128)(2,1)}) %all-reduce.2.cloned.1.call-update) | async-done | bytes 1048592 | tf_op jit(solution)/shard_map/psum | solution.py:110
  715.0 5.4 convert_bitcast_fusion.2
  720.4 9.2 %convert_bitcast_fusion.1 = bf16[16,2,2,2,16,16,16]{6,5,3,2,4,1,0:T(8,128)(2,1)} fusion(bf16[32,2,16,1,1,1,1]{0,2,1,6,5,4,3:T(8,128)(2,1)S(1)} %bitcast.138, bf16[32,2,16,1,1,1]{0,2,1,5,4,3:T(8,128)(2,1)S(1)} %bitcast.139, bf16[16,2,16,32,32,1]{4,2,1,3,0,5:T(8,128)(2,1)} %convert_bitcast_fusion.2), kind=kOutput, calls=%fused_computation.20 | convolution fusion | flops 68157440 | bytes 2101248 | tf_op jit(solution)/shard_map/xmezhw,wbf->xmezhbf/dot_general | solution.py:33
  729.6 9.1 %copy.59 = bf16[16,2,2,2,16,16,16]{6,5,4,3,2,1,0:T(8,128)(2,1)} copy(bf16[16,2,2,2,16,16,16]{6,5,3,2,4,1,0:T(8,128)(2,1)} %convert_bitcast_fusion.1) | data formatting | bytes 2097152 | tf_op jit(solution)/shard_map/convert_element_type | solution.py:35
  738.7 15.1 %reshape.75 = bf16[16,8,4096]{2,1,0:T(8,128)(2,1)S(1)} reshape(bf16[16,2,2,2,16,16,16]{6,5,4,3,2,1,0:T(8,128)(2,1)} %copy.59) | data formatting | bytes 2097152 | tf_op jit(solution)/shard_map/reshape | solution.py:37
  (63 shorter events, 45.4 us)
Async XLA Ops:
  6.5 14.5 %copy-start = (bf16[27,30720]{1,0:T(8,128)(2,1)S(1)}, bf16[27,30720]{1,0:T(8,128)(2,1)}, u32[]{:S(2)}) copy-start(bf16[27,30720]{1,0:T(8,128)(2,1)} %param.12) | copy-start | bytes 4976644
  11.5 12.0 %all-to-all-start.1 = ((bf16[8,2,8192]{2,1,0:T(2,128)(2,1)}), bf16[8,2,8192]{2,1,0:T(2,128)(2,1)S(1)}, u32[]{:S(2)}, u32[]{:S(2)}) async-start(bf16[8,2,8192]{2,1,0:T(2,128)(2,1)} %reshape.127), calls=%async_computation.1 | async-start | bytes 524288 | tf_op jit(solution)/shard_map/all_to_all | solution.py:64
  23.5 189.0 %all-to-all-start = ((s32[64,1,2]{2,1,0:T(1,128)}), s32[64,1,2]{2,1,0:T(1,128)S(1)}, u32[]{:S(2)}, u32[]{:S(2)}) async-start(s32[64,1,2]{2,1,0:T(1,128)} %bitcast.16), calls=%async_computation | async-start | bytes 65536 | tf_op jit(solution)/shard_map/all_to_all | solution.py:94
  212.5 385.1 %all-to-all-start.2 = ((bf16[64,2,32768]{2,1,0:T(2,128)(2,1)}), bf16[64,2,32768]{2,1,0:T(2,128)(2,1)}, u32[]{:S(2)}, u32[]{:S(2)}) async-start(bf16[64,2,32768]{2,1,0:T(2,128)(2,1)} %reshape.72), calls=%async_computation.2 | async-start | bytes 16777216 | tf_op jit(solution)/shard_map/all_to_all | solution.py:87
  227.8 487.2 %all-reduce.2.cloned.1.call-start = ((), (), s32[]{:S(2)}) async-start(), calls=%async_computation.3 | async-start | bytes 8388608 | tf_op jit(solution)/shard_map/psum | solution.py:110
  729.6 25.3 %copy-start.1 = (bf16[27,30720]{1,0:T(8,128)(2,1)S(1)}, bf16[27,30720]{1,0:T(8,128)(2,1)}, u32[]{:S(2)}) copy-start(bf16[27,30720]{1,0:T(8,128)(2,1)} %param.12) | copy-start | bytes 4976644
Sparse Core Ops, SparseCore 0:
  635.5 79.4 all-reduce.1
where the time goes:
time: 771 us; the launch traced here: 762 us
  waiting for transfers between devices  449 us (58%)
  matrix products  149 us (19%)
  local copies, waits for them, and re-layouts  105 us (14%)
  starting transfers between devices  38.4 us (5%)
  between operations  13.7 us (2%)
    all_to_all x1, waiting for transfers between devices, local(): lax.all_to_all(packed_rows.reshape(leaf_count, slot_count, cube_len), 'le...  369 us
    dot_general x4, matrix products, apply_parent(): jnp.einsum('ktabd,kteb->ktaed', section_z, factor_set[:, 1], preferred_el...  84 us
    psum x1, waiting for transfers between devices, local(): node_totals = lax.psum(partial_totals.astype(jnp.bfloat16), 'oct')  79.6 us
    dot_general x4, matrix products, apply_parent(): jnp.einsum('ktaed,ktfa->kfed', section_y, factor_set[:, 0], preferred_ele...  35.2 us
    reshape x1, local copies, waits for them, and re-layouts, local(): arrived.reshape(-1, cube_len)  22.7 us
    all_to_all x1, starting transfers between devices, local(): lax.all_to_all(packed_ids.reshape(leaf_count, slot_count), 'leaf', split_...  18.7 us
  transfers between devices with their start and end apart: 4, of which 2 were waited for; matrix products, arithmetic and copies ran while one was open for 23% of the time, Pallas kernels for 0%

commit v1 on v0

v1 whole, which is shorter than its diff:
```python
import functools

import jax
import jax.numpy as jnp
from jax import lax
from jax.experimental import pallas as pl
from jax.experimental.pallas import tpu as pltpu
from jax.sharding import PartitionSpec as P

BF = jnp.bfloat16
F32 = jnp.float32
MESH = pl.DeviceIdType.MESH
VM = pl.BlockSpec(memory_space=pltpu.VMEM)
NT = (((1,), (1,)), ((), ()))
NN = (((1,), (0,)), ((), ()))
NY, NZ, NO = 4, 16, 8
SUBS = 4


def mm(a, b, dims=NN):
    return lax.dot_general(a, b, dims, preferred_element_type=F32)


def exchange_kernel(slot_ref, ch_ref, out_ref, stage, send_sem, recv_sem):
    leaf, octant = lax.axis_index("leaf"), lax.axis_index("oct")
    barrier = pltpu.get_barrier_semaphore()
    for d in range(1, NO):
        pl.semaphore_signal(
            barrier, inc=1, device_id=(leaf, lax.rem(octant + d, NO)), device_id_type=MESH
        )
    for q in range(32):
        stage[q // 4, q % 4] = ch_ref[slot_ref[q]]
    pl.semaphore_wait(barrier, NO - 1)
    copies = []
    for d in range(1, NO):
        target = lax.rem(octant + d, NO)
        copy = pltpu.make_async_remote_copy(
            src_ref=stage.at[target],
            dst_ref=out_ref.at[octant],
            send_sem=send_sem.at[d],
            recv_sem=recv_sem.at[d],
            device_id=(leaf, target),
            device_id_type=MESH,
        )
        copy.start()
        copies.append(copy)
    out_ref[octant] = stage[octant]
    for copy in copies:
        copy.wait()


def exchange(slots, child_cubes):
    return pl.pallas_call(
        exchange_kernel,
        out_shape=jax.ShapeDtypeStruct((NO, 4, 16, 256), BF),
        in_specs=[pl.BlockSpec(memory_space=pltpu.SMEM), VM],
        out_specs=VM,
        scratch_shapes=[
            pltpu.VMEM((NO, 4, 16, 256), BF),
            pltpu.SemaphoreType.DMA((NO,)),
            pltpu.SemaphoreType.DMA((NO,)),
        ],
        compiler_params=pltpu.CompilerParams(collective_id=0, has_side_effects=True),
        name="exchange",
    )(slots, child_cubes)


def apply_kernel(
    b_ref, f_ref, w_ref, wt_ref, wtd_ref, wc4_ref, bd_ref, out_ref,
    mask2, mask3, s1, base2, base3, lhs3, e3, totals,
):
    row = lax.broadcasted_iota(jnp.int32, (256, 256), 0)
    col = lax.broadcasted_iota(jnp.int32, (256, 256), 1)
    mask2[...] = jnp.where(col % 8 == (row // 16) % 8, 1.0, 0.0).astype(BF)
    mask3[...] = jnp.where(col % 8 == (row // 8) % 8, 1.0, 0.0).astype(BF)

    def entry(n, carry):
        p = n // 4
        x_rows = []
        for i in range(2):
            tiles = []
            for j in range(2):
                for vh in range(2):
                    for l in range(2):
                        tiles.append(b_ref[4 * i + 2 * j + l, p, :, vh * 128:(vh + 1) * 128])
            x_rows.append(jnp.concatenate(tiles, axis=1))
        x = jnp.concatenate(x_rows, axis=0)
        g0 = mm(f_ref[n, 0:320, :], w_ref[...]).astype(BF)
        h0 = mm(bd_ref[...], g0).astype(BF)
        s1[...] = mm(h0, x).astype(BF)
        a1 = mm(wtd_ref[...], f_ref[n, 320:640, :], NT).astype(BF)
        a2 = mm(wt_ref[...], f_ref[n, 640:960, :], NT).astype(BF)
        for g, width in ((0, 128), (1, 128), (2, 64)):
            ins = slice(g * 128, g * 128 + width)
            outs = slice(g * 1024, g * 1024 + width * 8)
            base3[:, outs] = mm(a1[:, ins], wc4_ref[0:width, 0:width * 8]).astype(BF)
            base2[:, outs] = mm(a2[:, ins], wc4_ref[0:width, 0:width * 8]).astype(BF)
        for t in range(10):
            lanes = slice(t * 256, (t + 1) * 256)
            for bh in range(4):
                for cp in range(4):
                    r = bh * 64 + cp * 16
                    e3[t * 256 + r:t * 256 + r + 16, :] = (
                        base3[bh * 16:(bh + 1) * 16, lanes] * mask3[r:r + 16, :]
                    )
            e2 = jnp.concatenate(
                [base2[0:16, lanes]] * 8 + [base2[16:32, lanes]] * 8, axis=0
            ) * mask2[...]
            lhs2 = jnp.concatenate(
                [s1[t * 32:(t + 1) * 32, bh * 256:(bh + 1) * 256] for bh in range(4)], axis=0
            )
            mid = mm(lhs2, e2)
            for ch in range(4):
                lhs3[ch * 32:(ch + 1) * 32, lanes] = jnp.concatenate(
                    [mid[bh * 32:(bh + 1) * 32, ch * 64:(ch + 1) * 64] for bh in range(4)], axis=1
                ).astype(BF)
        total = mm(lhs3[...], e3[...])
        for i in range(2):
            for j in range(2):
                for l in range(2):
                    for wh in range(2):
                        r = (2 * l + wh) * 32 + i * 16
                        start = pl.multiple_of(n * 32 + wh * 16, 16)
                        totals[4 * i + 2 * j + l, pl.ds(start, 16), :] = total[
                            r:r + 16, j * 128:(j + 1) * 128
                        ]
        return carry

    lax.fori_loop(0, 16, entry, 0)

    def spread(o, carry):
        for r in range(32):
            out_ref[o, r] = totals[o, pl.ds(r, 16, stride=32), :].astype(BF)
        return carry

    lax.fori_loop(0, NO, spread, 0)


def apply_entries(blocks, kind_factors, two_scale):
    wt = two_scale.T
    wtd = jnp.broadcast_to(wt.reshape(4, 1, 8, 32), (4, 2, 8, 32)).reshape(64, 32)
    wc = jnp.repeat(two_scale, 8, axis=1)
    wc4 = jnp.kron(jnp.eye(4, dtype=BF), wc)
    bd = jnp.kron(jnp.eye(10, dtype=BF), wt)
    return pl.pallas_call(
        apply_kernel,
        out_shape=jax.ShapeDtypeStruct((NO, 32, 16, 128), BF),
        in_specs=[VM] * 7,
        out_specs=VM,
        scratch_shapes=[
            pltpu.VMEM((256, 256), BF),
            pltpu.VMEM((256, 256), BF),
            pltpu.VMEM((320, 1024), BF),
            pltpu.VMEM((32, 2560), BF),
            pltpu.VMEM((64, 2560), BF),
            pltpu.VMEM((128, 2560), BF),
            pltpu.VMEM((2560, 256), BF),
            pltpu.VMEM((NO, 512, 128), F32),
        ],
        compiler_params=pltpu.CompilerParams(vmem_limit_bytes=48 << 20),
        name="apply_entries",
    )(blocks, kind_factors, two_scale, wt, wtd, wc4, bd)


def deliver_kernel(
    c_ref, id_ref, out_ref, rows, idx, idy, part, from_low, from_high,
    xs, xr, ixs, ixr, ys, yr, fs, fr, iys, iyr, ps, pr, ms, mr,
):
    leaf, octant = lax.axis_index("leaf"), lax.axis_index("oct")
    z, y = leaf // NY, lax.rem(leaf, NY)

    def at_y(d):
        return (z * NY + lax.rem(y + d, NY), octant)

    up_z = (lax.rem(z + 1, NZ) * NY + y, octant)
    down_z = (lax.rem(z + NZ - 1, NZ) * NY + y, octant)

    def remote(src, dst, ss, rs, where):
        copy = pltpu.make_async_remote_copy(
            src_ref=src, dst_ref=dst, send_sem=ss, recv_sem=rs, device_id=where,
            device_id_type=MESH,
        )
        copy.start()
        return copy

    barrier = pltpu.get_barrier_semaphore()
    partners = [(leaf, lax.rem(octant + d, NO)) for d in range(1, NO)]
    partners += [at_y(1), at_y(2), at_y(3), up_z, down_z]
    for partner in partners:
        pl.semaphore_signal(barrier, inc=1, device_id=partner, device_id_type=MESH)
    pl.semaphore_wait(barrier, len(partners))

    x_copies, ix_copies = [], []
    for d in range(1, NO):
        target = lax.rem(octant + d, NO)
        where = (leaf, target)
        ix_copies.append(remote(id_ref, idx.at[octant], ixs.at[d], ixr.at[d], where))
        x_copies.append(
            remote(c_ref.at[target], rows.at[y, octant], xs.at[d], xr.at[d], where)
        )
    rows[y, octant] = c_ref[octant]
    idx[octant] = id_ref[...]

    y_copies = []

    def send_y(d):
        source = lax.rem(octant + NO - d, NO)
        block = rows.at[y, source]
        y_copies.append((
            remote(block, block, ys.at[0, d], yr.at[0, d], at_y(1)),
            remote(block, block, ys.at[1, d], yr.at[1, d], at_y(3)),
        ))

    send_y(0)
    for copy in ix_copies:
        copy.wait()
    idy[y] = jnp.sum(idx[...], axis=0)
    iy_copies = [
        remote(idy.at[y], idy.at[y], iys.at[d], iyr.at[d], at_y(d)) for d in range(1, NY)
    ]
    f_copies = []

    def forward(d):
        source = lax.rem(octant + NO - d, NO)
        up, down = y_copies[d]
        up.wait_recv()
        down.wait_recv()
        if d < 4:
            block = rows.at[lax.rem(y + NY - 1, NY), source]
            f_copies.append(remote(block, block, fs.at[d], fr.at[d], at_y(1)))
        else:
            block = rows.at[lax.rem(y + 1, NY), source]
            f_copies.append(remote(block, block, fs.at[d], fr.at[d], at_y(3)))

    for d in range(1, NO):
        x_copies[d - 1].wait()
        send_y(d)
    for d in range(NO):
        forward(d)
    for copy in iy_copies:
        copy.wait()
    for copy in f_copies:
        copy.wait()
    for up, down in y_copies:
        up.wait_send()
        down.wait_send()

    rho = lax.broadcasted_iota(jnp.int32, (256, 128), 0)
    key = (rho // 16) * 64 + y * 16 + rho % 16
    select = jnp.concatenate(
        [jnp.where(key == idy[s][0:1, :], 1.0, 0.0).astype(BF) for s in range(NY)], axis=1
    )

    def node_sums(r, carry):
        lo = rows[:, :, 2 * r].reshape(512, 128)
        hi = rows[:, :, 2 * r + 1].reshape(512, 128)
        sums = mm(select, jnp.concatenate([lo, hi], axis=1)).astype(BF)
        part[:, 2 * r] = sums[:, 0:128].reshape(NZ, 16, 128)
        part[:, 2 * r + 1] = sums[:, 128:256].reshape(NZ, 16, 128)
        return carry

    lax.fori_loop(0, 16, node_sums, 0)

    width = 32 // SUBS
    up_copies, down_copies = {}, {}
    for s in range(8):
        high = lax.rem(z + 8 - s, NZ)
        low = lax.rem(z + NZ - 7 + s, NZ)
        for u in range(SUBS):
            span = pl.ds(u * width, width)
            if s > 0:
                up_copies[s - 1, u].wait_recv()
                part[high, span] = part[high, span] + from_low[s - 1, span]
            up_copies[s, u] = remote(
                part.at[high, span], from_low.at[s, span], ps.at[s, u], pr.at[s, u], up_z
            )
            if s < 7:
                if s > 0:
                    down_copies[s - 1, u].wait_recv()
                    part[low, span] = part[low, span] + from_high[s - 1, span]
                down_copies[s, u] = remote(
                    part.at[low, span], from_high.at[s, span], ms.at[s, u], mr.at[s, u], down_z
                )
    row = lax.broadcasted_iota(jnp.int32, (256, 256), 0)
    col = lax.broadcasted_iota(jnp.int32, (256, 256), 1)
    source_lane = (col % 16) // 8 * 128 + (col // 16) * 8 + col % 8
    perm = jnp.where(row == source_lane, 1.0, 0.0).astype(BF)
    for u in range(SUBS):
        down_copies[6, u].wait_recv()
        up_copies[7, u].wait_recv()
    for u in range(16):
        pieces = []
        for wh in range(2):
            r = wh * 16 + u
            pieces.append((
                part[z, r].astype(F32) + from_low[7, r].astype(F32) + from_high[6, r].astype(F32)
            ).astype(BF))
        out_ref[:, u * 256:(u + 1) * 256] = mm(
            jnp.concatenate(pieces, axis=1), perm
        ).astype(BF)
    for copy in list(up_copies.values()) + list(down_copies.values()):
        copy.wait_send()


def deliver(pieces, ids):
    dma = pltpu.SemaphoreType.DMA
    return pl.pallas_call(
        deliver_kernel,
        out_shape=jax.ShapeDtypeStruct((16, 4096), BF),
        in_specs=[VM, VM],
        out_specs=VM,
        scratch_shapes=[
            pltpu.VMEM((NY, NO, 32, 16, 128), BF),
            pltpu.VMEM((NO, 8, 128), jnp.int32),
            pltpu.VMEM((NY, 8, 128), jnp.int32),
            pltpu.VMEM((NZ, 32, 16, 128), BF),
            pltpu.VMEM((8, 32, 16, 128), BF),
            pltpu.VMEM((7, 32, 16, 128), BF),
            dma((NO,)), dma((NO,)), dma((NO,)), dma((NO,)),
            dma((2, NO)), dma((2, NO)), dma((NO,)), dma((NO,)), dma((NY,)), dma((NY,)),
            dma((8, SUBS)), dma((8, SUBS)), dma((7, SUBS)), dma((7, SUBS)),
        ],
        compiler_params=pltpu.CompilerParams(
            collective_id=1, has_side_effects=True, vmem_limit_bytes=48 << 20
        ),
        name="deliver",
    )(pieces, ids)


def local(children, child_slot, two_scale, factors, disp_kind, target_leaf, target_node):
    kind_factors = factors[disp_kind.reshape(-1)].reshape(16, 960, 32)
    blocks = exchange(child_slot.reshape(-1), children.reshape(32, 16, 256))
    pieces = apply_entries(blocks, kind_factors, two_scale)
    goal = target_leaf.reshape(-1) * 16 + target_node.reshape(-1)
    lane = jnp.arange(128, dtype=jnp.int32)
    ids = jnp.where(lane // 16 == lax.axis_index("oct"), jnp.tile(goal, 8), 0)
    ids = jnp.broadcast_to(ids[None, :], (8, 128))
    return deliver(pieces, ids).reshape(16, 1, 4096)


def solution(mesh):
    placed = (
        P(("leaf", "oct"), None),
        P("leaf", "oct"),
        P(),
        P(),
        P(("leaf", "oct"), None),
        P(("leaf", "oct"), None, None),
        P(("leaf", "oct"), None),
    )
    return jax.shard_map(
        local, mesh=mesh, in_specs=placed, out_specs=P("leaf", "oct", None), check_vma=False
    )
```

time: 771 us -> 143 us (0.19)
  the two profiles are of different devices: /device:TPU:8 before, /device:TPU:2 now
where the time goes in v1:
time: 143 us
  Pallas kernels  128 us (90%)
  local copies, waits for them, and re-layouts  13.8 us (10%)
    pallas_call x1, Pallas kernels, deliver(): pl.pallas_call(deliver_kernel, out_shape=jax.ShapeDtypeStruct((16, 4096),...  87.3 us
    pallas_call x1, Pallas kernels, apply_entries(): pl.pallas_call(apply_kernel, out_shape=jax.ShapeDtypeStruct((NO, 32, 16,...  28 us
    pallas_call x1, Pallas kernels, exchange(): pl.pallas_call(exchange_kernel, out_shape=jax.ShapeDtypeStruct((NO, 4, 16...  13.2 us
    unnamed x16, local copies, waits for them, and re-layouts  6.37 us
    reshape x2, local copies, waits for them, and re-layouts, local(): kind_factors = factors[disp_kind.reshape(-1)].reshape(16, 960, 32)  4.49 us

profile of v1, /device:TPU:2, one launch (start us, length us, event | category | flops | bytes accessed | tf_op | source)
XLA Modules:
  0.0 142.8 jit_solution(2476952236122267404)
XLA Ops:
  0.0 0.0 copy-start
  0.0 0.9 copy.9
  0.9 0.2 broadcast_multiply_fusion
  1.1 0.0 copy-start.4
  1.1 0.7 mul.68.bd_ref
  1.9 0.1 copy.11
  2.0 0.2 broadcast_multiply_fusion.1
  2.2 0.0 copy-done.4
  2.2 0.1 reshape.115
  2.3 0.0 copy-done
  2.3 1.2 gather_fusion
  3.5 0.0 copy-start.3
  3.5 4.4 %reshape.116.f_ref = bf16[16,960,32]{2,1,0:T(8,128)(2,1)} reshape(bf16[16,30720]{1,0:T(8,128)(2,1)S(1)} %gather_fusion) | data formatting | bytes 1966080 | tf_op jit(solution)/shard_map/reshape | solution.py:331
  7.9 1.7 %copy.12 = bf16[4,8,16,256]{3,2,1,0:T(8,128)(2,1)} copy(bf16[4,8,16,256]{3,1,2,0:T(8,128)(2,1)} %bitcast.23) | data formatting | bytes 524288
  9.6 13.2 %exchange.1.b_ref = bf16[8,4,16,256]{3,2,1,0:T(8,128)(2,1)} custom-call(s32[32]{0:T(128)} %bitcast.24, bf16[32,16,256]{2,1,0:T(8,128)(2,1)} %bitcast.21), custom_call_target="tpu_custom_call" | custom-call | tf_op jit(solution)/shard_map/exchange/pallas_call | solution.py:53
  22.8 0.0 copy-done.3
  22.8 2.1 %copy-done.1 = bf16[16,960,32]{2,1,0:T(8,128)(2,1)S(1)} copy-done((bf16[16,960,32]{2,1,0:T(8,128)(2,1)S(1)}, bf16[16,960,32]{2,1,0:T(8,128)(2,1)}, u32[]{:S(2)}) %copy-start.1) | copy-done | bytes 983064
  24.9 0.9 copy-done.2
  25.9 28.0 %apply_entries.1.c_ref = bf16[8,32,16,128]{3,2,1,0:T(8,128)(2,1)S(1)} custom-call(bf16[8,4,16,256]{3,2,1,0:T(8,128)(2,1)S(1)} %copy-done.2, bf16[16,960,32]{2,1,0:T(8,128)(2,1)S(1)} %copy-done.1, bf16[32,32]{1,0:T(8,128)(2,1)S(1)} %copy-done.3, bf16[32,32]{1,0:T(8,128)(2,1)S(1)} %bitcast.19, bf16[64,32]{1,0:T(8,128)(2,1)S(1)} %bitcast.20, ...), custom_call_target="tpu_custom_call" | custom-call | tf_op jit(solution)/shard_map/apply_entries/pallas_call | solution.py:145
  53.9 0.1 mul.70
  53.9 0.8 reshape.118
  54.7 0.1 tile.10
  54.8 87.3 %deliver.1 = bf16[16,4096]{1,0:T(8,128)(2,1)S(1)} custom-call(bf16[8,32,16,128]{3,2,1,0:T(8,128)(2,1)S(1)} %apply_entries.1.c_ref, s32[8,128]{1,0:T(8,128)S(1)} %broadcast_in_dim.30.id_ref), custom_call_target="tpu_custom_call" | custom-call | tf_op jit(solution)/shard_map/deliver/pallas_call | solution.py:307
  142.1 0.7 copy.15
  (16 shorter events, 0.1 us)
Async XLA Ops:
  0.0 2.3 %copy-start = (bf16[27,30720]{1,0:T(8,128)(2,1)S(1)}, bf16[27,30720]{1,0:T(8,128)(2,1)}, u32[]{:S(2)}) copy-start(bf16[27,30720]{1,0:T(8,128)(2,1)} %param.10) | copy-start | bytes 4976644
  1.1 1.1 copy-start.4
  3.5 19.3 %copy-start.3 = (bf16[32,32]{1,0:T(8,128)(2,1)S(1)}, bf16[32,32]{1,0:T(8,128)(2,1)}, u32[]{:S(2)}) copy-start(bf16[32,32]{1,0:T(8,128)(2,1)} %w_ref.1) | copy-start | bytes 6148
  22.8 2.1 %copy-start.1 = (bf16[16,960,32]{2,1,0:T(8,128)(2,1)S(1)}, bf16[16,960,32]{2,1,0:T(8,128)(2,1)}, u32[]{:S(2)}) copy-start(bf16[16,960,32]{2,1,0:T(8,128)(2,1)} %reshape.116.f_ref) | copy-start | bytes 2949124
  24.9 0.9 copy-start.2
  25.9 28.0 %copy-start.5 = (s32[4,4,1]{1,2,0:T(1,128)S(1)}, s32[4,4,1]{1,2,0:T(1,128)}, u32[]{:S(2)}) copy-start(s32[4,4,1]{1,2,0:T(1,128)} %param.12) | copy-start | bytes 196

commit v2 on v0

v2 whole, which is shorter than its diff:
```python
import functools

import jax
import jax.numpy as jnp
from jax import lax
from jax.experimental import pallas as pl
from jax.experimental.pallas import tpu as pltpu
from jax.sharding import PartitionSpec as P

BF = jnp.bfloat16
F32 = jnp.float32
MESH = pl.DeviceIdType.MESH
VM = pl.BlockSpec(memory_space=pltpu.VMEM)
NT = (((1,), (1,)), ((), ()))
NN = (((1,), (0,)), ((), ()))
NY, NZ, NO = 4, 16, 8
SUBS = 4
NP = 4


def mm(a, b, dims=NN):
    return lax.dot_general(a, b, dims, preferred_element_type=F32)


def apply_all_kernel(
    slot_ref, kind_ref, ch_ref, tab_ref, w_ref, wt_ref, wtd_ref, wc4_ref, bd_ref, id_ref, out_ref,
    stage, blocks, mask2, mask3, flat, h0s, base2, base3, s1, lhs3, e3, totals, pieces,
    rows, idx, idy, select, acc, part, from_low, from_high,
    es, er, xs, xr, ixs, ixr, ys, yr, fs, fr, iys, iyr, ps, pr, ms, mr,
):
    leaf, octant = lax.axis_index("leaf"), lax.axis_index("oct")
    z, y = leaf // NY, lax.rem(leaf, NY)

    def at_y(d):
        return (z * NY + lax.rem(y + d, NY), octant)

    up_z = (lax.rem(z + 1, NZ) * NY + y, octant)
    down_z = (lax.rem(z + NZ - 1, NZ) * NY + y, octant)
    targets = [lax.rem(octant + d, NO) for d in range(NO)]

    def remote(src, dst, ss, rs, where):
        copy = pltpu.make_async_remote_copy(
            src_ref=src, dst_ref=dst, send_sem=ss, recv_sem=rs, device_id=where,
            device_id_type=MESH,
        )
        copy.start()
        return copy

    barrier = pltpu.get_barrier_semaphore()
    partners = [(leaf, targets[d]) for d in range(1, NO)]
    partners += [at_y(1), at_y(2), at_y(3), up_z, down_z]
    for partner in partners:
        pl.semaphore_signal(barrier, inc=1, device_id=partner, device_id_type=MESH)
    for q in range(32):
        stage[q // 4, q % 4] = ch_ref[slot_ref[q]]
    idx[octant] = id_ref[...]
    pl.semaphore_wait(barrier, len(partners))

    e_copies, ix_copies = [], []
    for d in range(1, NO):
        where = (leaf, targets[d])
        e_copies.append(
            remote(stage.at[targets[d]], blocks.at[octant], es.at[d], er.at[d], where)
        )
    for d in range(1, NO):
        where = (leaf, targets[d])
        ix_copies.append(remote(id_ref, idx.at[octant], ixs.at[d], ixr.at[d], where))
    blocks[octant] = stage[octant]

    row = lax.broadcasted_iota(jnp.int32, (256, 256), 0)
    col = lax.broadcasted_iota(jnp.int32, (256, 256), 1)
    mask2[...] = jnp.where(col % 8 == (row // 16) % 8, 1.0, 0.0).astype(BF)
    mask3[...] = jnp.where(col % 8 == (row // 8) % 8, 1.0, 0.0).astype(BF)

    def fold(n, carry):
        dense = tab_ref[kind_ref[n]].astype(F32)
        for o in range(4):
            flat[pl.ds(o, 240, stride=4), :] = dense[:, o * 32:(o + 1) * 32]
        g0 = mm(flat[0:320, :].astype(BF), w_ref[...]).astype(BF)
        h0s[n] = mm(bd_ref[...], g0).astype(BF)
        a1 = mm(wtd_ref[...], flat[320:640, :].astype(BF), NT).astype(BF)
        a2 = mm(wt_ref[...], flat[640:960, :].astype(BF), NT).astype(BF)
        for g, width in ((0, 128), (1, 128), (2, 64)):
            ins = slice(g * 128, g * 128 + width)
            outs = slice(g * 1024, g * 1024 + width * 8)
            base3[n, :, outs] = mm(a1[:, ins], wc4_ref[0:width, 0:width * 8]).astype(BF)
            base2[n, :, outs] = mm(a2[:, ins], wc4_ref[0:width, 0:width * 8]).astype(BF)
        return carry

    lax.fori_loop(0, 16, fold, 0)
    for copy in e_copies:
        copy.wait()

    x_copies, y_copies, f_copies = {}, {}, {}

    def send_x(p):
        for d in range(1, NO):
            x_copies[p, d] = remote(
                pieces.at[p, targets[d]], rows.at[y, p, octant], xs.at[p, d], xr.at[p, d],
                (leaf, targets[d]),
            )
        rows[y, p, octant] = pieces[p, octant]

    def send_y(p):
        for d in range(1, NO):
            x_copies[p, d].wait_recv()
        block = rows.at[y, p]
        y_copies[p] = (
            remote(block, block, ys.at[0, p], yr.at[0, p], at_y(1)),
            remote(block, block, ys.at[1, p], yr.at[1, p], at_y(3)),
        )

    def forward(p):
        up, down = y_copies[p]
        up.wait_recv()
        block = rows.at[lax.rem(y + NY - 1, NY), p, 0:4]
        first = remote(block, block, fs.at[0, p], fr.at[0, p], at_y(1))
        down.wait_recv()
        block = rows.at[lax.rem(y + 1, NY), p, 4:8]
        second = remote(block, block, fs.at[1, p], fr.at[1, p], at_y(3))
        f_copies[p] = (first, second)

    iy_copies = []
    for p in range(NP):
        x_rows = []
        for i in range(2):
            tiles = []
            for j in range(2):
                for vh in range(2):
                    for l in range(2):
                        tiles.append(blocks[4 * i + 2 * j + l, p, :, vh * 128:(vh + 1) * 128])
            x_rows.append(jnp.concatenate(tiles, axis=1))
        x = jnp.concatenate(x_rows, axis=0)

        def entry(k, carry):
            n = p * 4 + k
            s1[...] = mm(h0s[n], x).astype(BF)
            for t in range(10):
                lanes = slice(t * 256, (t + 1) * 256)
                for bh in range(4):
                    tile = base3[n, bh * 16:(bh + 1) * 16, lanes]
                    for cp in range(4):
                        r = bh * 64 + cp * 16
                        e3[t * 256 + r:t * 256 + r + 16, :] = tile * mask3[r:r + 16, :]
                low, high = base2[n, 0:16, lanes], base2[n, 16:32, lanes]
                e2 = jnp.concatenate([low] * 8 + [high] * 8, axis=0) * mask2[...]
                lhs2 = jnp.concatenate(
                    [s1[t * 32:(t + 1) * 32, bh * 256:(bh + 1) * 256] for bh in range(4)], axis=0
                )
                mid = mm(lhs2, e2)
                for ch in range(4):
                    lhs3[ch * 32:(ch + 1) * 32, lanes] = jnp.concatenate(
                        [mid[bh * 32:(bh + 1) * 32, ch * 64:(ch + 1) * 64] for bh in range(4)],
                        axis=1,
                    ).astype(BF)
            total = mm(lhs3[...], e3[...])
            for i in range(2):
                for j in range(2):
                    for l in range(2):
                        for wh in range(2):
                            r = (2 * l + wh) * 32 + i * 16
                            start = pl.multiple_of(k * 32 + wh * 16, 16)
                            totals[4 * i + 2 * j + l, pl.ds(start, 16), :] = total[
                                r:r + 16, j * 128:(j + 1) * 128
                            ]
            return carry

        lax.fori_loop(0, 3, entry, 0)
        if p == 0:
            for copy in ix_copies:
                copy.wait()
            idy[y] = jnp.sum(idx[...], axis=0)
            for d in range(1, NY):
                iy_copies.append(remote(idy.at[y], idy.at[y], iys.at[d], iyr.at[d], at_y(d)))
        if p >= 1:
            send_y(p - 1)
        lax.fori_loop(3, 4, entry, 0)
        for o in range(NO):
            for r in range(8):
                pieces[p, o, r] = totals[o, pl.ds(r, 16, stride=8), :].astype(BF)
        send_x(p)
        if p >= 2:
            forward(p - 2)

    rho = lax.broadcasted_iota(jnp.int32, (256, 128), 0)
    key = (rho // 16) * 64 + y * 16 + rho % 16
    lane = lax.broadcasted_iota(jnp.int32, (256, 128), 1)

    def node_sums(p):
        for h in range(4):
            for s in range(NY):
                hit = (key == idy[s, p:p + 1, :]) & (lane % 4 == h)
                select[h, :, s * 128:(s + 1) * 128] = jnp.where(hit, 1.0, 0.0).astype(BF)
        for copy in f_copies[p]:
            copy.wait_recv()

        def two_rows(r, carry):
            lo = rows[:, p, :, 2 * r].reshape(512, 128)
            hi = rows[:, p, :, 2 * r + 1].reshape(512, 128)
            both = jnp.concatenate([lo, hi], axis=1)
            for h in range(4):
                new = mm(select[h], both)
                if p > 0:
                    new = new + acc[h, r]
                if p < NP - 1:
                    acc[h, r] = new
                else:
                    new = new.astype(BF)
                    part[:, h * 8 + 2 * r] = new[:, 0:128].reshape(NZ, 16, 128)
                    part[:, h * 8 + 2 * r + 1] = new[:, 128:256].reshape(NZ, 16, 128)
            return carry

        lax.fori_loop(0, 4, two_rows, 0)

    for copy in iy_copies:
        copy.wait()
    node_sums(0)
    send_y(3)
    forward(2)
    node_sums(1)
    forward(3)
    node_sums(2)
    node_sums(3)

    width = 32 // SUBS
    up_copies, down_copies = {}, {}
    for s in range(8):
        high = lax.rem(z + 8 - s, NZ)
        low = lax.rem(z + NZ - 7 + s, NZ)
        for u in range(SUBS):
            span = pl.ds(u * width, width)
            if s > 0:
                up_copies[s - 1, u].wait_recv()
                part[high, span] = part[high, span] + from_low[s - 1, span]
            up_copies[s, u] = remote(
                part.at[high, span], from_low.at[s, span], ps.at[s, u], pr.at[s, u], up_z
            )
            if s < 7:
                if s > 0:
                    down_copies[s - 1, u].wait_recv()
                    part[low, span] = part[low, span] + from_high[s - 1, span]
                down_copies[s, u] = remote(
                    part.at[low, span], from_high.at[s, span], ms.at[s, u], mr.at[s, u], down_z
                )
    row = lax.broadcasted_iota(jnp.int32, (256, 256), 0)
    col = lax.broadcasted_iota(jnp.int32, (256, 256), 1)
    source_lane = (col % 16) // 8 * 128 + (col // 16) * 8 + col % 8
    perm = jnp.where(row == source_lane, 1.0, 0.0).astype(BF)
    for u in range(SUBS):
        down_copies[6, u].wait_recv()
        up_copies[7, u].wait_recv()
    for u in range(16):
        pair = []
        for wh in range(2):
            r = wh * 16 + u
            pair.append((
                part[z, r].astype(F32) + from_low[7, r].astype(F32) + from_high[6, r].astype(F32)
            ).astype(BF))
        out_ref[:, u * 256:(u + 1) * 256] = mm(
            jnp.concatenate(pair, axis=1), perm
        ).astype(BF)
    for copy in list(up_copies.values()) + list(down_copies.values()):
        copy.wait_send()
    for p in range(NP):
        for copy in f_copies[p] + y_copies[p]:
            copy.wait_send()
        for d in range(1, NO):
            x_copies[p, d].wait_send()


def apply_all(slots, kinds, child_cubes, table, two_scale, ids):
    dma = pltpu.SemaphoreType.DMA
    smem = pl.BlockSpec(memory_space=pltpu.SMEM)
    wt = two_scale.T
    wtd = jnp.broadcast_to(wt.reshape(4, 1, 8, 32), (4, 2, 8, 32)).reshape(64, 32)
    wc4 = jnp.kron(jnp.eye(4, dtype=BF), jnp.repeat(two_scale, 8, axis=1))
    bd = jnp.kron(jnp.eye(10, dtype=BF), wt)
    return pl.pallas_call(
        apply_all_kernel,
        out_shape=jax.ShapeDtypeStruct((16, 4096), BF),
        in_specs=[smem, smem] + [VM] * 8,
        out_specs=VM,
        scratch_shapes=[
            pltpu.VMEM((NO, NP, 16, 256), BF),
            pltpu.VMEM((NO, NP, 16, 256), BF),
            pltpu.VMEM((256, 256), BF),
            pltpu.VMEM((256, 256), BF),
            pltpu.VMEM((960, 32), F32),
            pltpu.VMEM((16, 320, 32), BF),
            pltpu.VMEM((16, 32, 2560), BF),
            pltpu.VMEM((16, 64, 2560), BF),
            pltpu.VMEM((320, 1024), BF),
            pltpu.VMEM((128, 2560), BF),
            pltpu.VMEM((2560, 256), BF),
            pltpu.VMEM((NO, 128, 128), F32),
            pltpu.VMEM((NP, NO, 8, 16, 128), BF),
            pltpu.VMEM((NY, NP, NO, 8, 16, 128), BF),
            pltpu.VMEM((NO, 8, 128), jnp.int32),
            pltpu.VMEM((NY, 8, 128), jnp.int32),
            pltpu.VMEM((4, 256, 512), BF),
            pltpu.VMEM((4, 4, 256, 256), F32),
            pltpu.VMEM((NZ, 32, 16, 128), BF),
            pltpu.VMEM((8, 32, 16, 128), BF),
            pltpu.VMEM((7, 32, 16, 128), BF),
            dma((NO,)), dma((NO,)), dma((NP, NO)), dma((NP, NO)), dma((NO,)), dma((NO,)),
            dma((2, NP)), dma((2, NP)), dma((2, NP)), dma((2, NP)), dma((NY,)), dma((NY,)),
            dma((8, SUBS)), dma((8, SUBS)), dma((7, SUBS)), dma((7, SUBS)),
        ],
        compiler_params=pltpu.CompilerParams(
            collective_id=0, has_side_effects=True, vmem_limit_bytes=56 << 20
        ),
        name="apply_all",
    )(slots, kinds, child_cubes, table, two_scale, wt, wtd, wc4, bd, ids)


def local(children, child_slot, two_scale, factors, disp_kind, target_leaf, target_node):
    goal = (target_leaf[:, :, 0] * 16 + target_node).astype(jnp.int32)
    lane = jnp.arange(128, dtype=jnp.int32)
    spread = jnp.tile(jnp.repeat(goal, 4, axis=1), (1, NO))
    ids = jnp.where(lane // 16 == lax.axis_index("oct"), spread, 0)
    out = apply_all(
        child_slot.reshape(-1), disp_kind.reshape(-1), children.reshape(32, 16, 256),
        factors.reshape(-1, 240, 128), two_scale, jnp.pad(ids, ((0, 4), (0, 0))),
    )
    return out.reshape(16, 1, 4096)


def solution(mesh):
    placed = (
        P(("leaf", "oct"), None),
        P("leaf", "oct"),
        P(),
        P(),
        P(("leaf", "oct"), None),
        P(("leaf", "oct"), None, None),
        P(("leaf", "oct"), None),
    )
    return jax.shard_map(
        local, mesh=mesh, in_specs=placed, out_specs=P("leaf", "oct", None), check_vma=False
    )
```

time: 771 us -> 119 us (0.15)
  the two profiles are of different devices: /device:TPU:8 before, /device:TPU:2 now
where the time goes in v2:
time: 119 us
  Pallas kernels  107 us (90%)
  local copies, waits for them, and re-layouts  11.5 us (10%)
    pallas_call x1, Pallas kernels, apply_all(): pl.pallas_call(apply_all_kernel, out_shape=jax.ShapeDtypeStruct((16, 4096...  107 us
    unnamed x13, local copies, waits for them, and re-layouts  5.91 us

profile of v2, /device:TPU:2, one launch (start us, length us, event | category | flops | bytes accessed | tf_op | source)
XLA Modules:
  0.0 118.6 jit_solution(18027561092587248498)
XLA Ops:
  0.0 1.3 %reshape.57.kind_ref = s32[16]{0:T(128)} reshape(s32[4,4]{1,0:T(4,128)} %param.11) | data formatting | bytes 128 | tf_op jit(solution)/shard_map/reshape | solution.py:322
  1.3 1.7 %copy.12 = bf16[4,8,16,256]{3,2,1,0:T(8,128)(2,1)} copy(bf16[4,8,16,256]{3,1,2,0:T(8,128)(2,1)} %bitcast.23) | data formatting | bytes 524288
  3.0 1.8 %copy.13 = bf16[4,8,240,128]{3,2,1,0:T(8,128)(2,1)S(1)} copy(bf16[4,8,240,128]{3,1,2,0:T(8,128)(2,1)} %bitcast.18) | data formatting | bytes 3932160
  4.8 0.0 copy-start.1
  4.9 1.3 %slice.tab_ref = bf16[27,240,128]{2,1,0:T(8,128)(2,1)} slice(bf16[32,240,128]{2,1,0:T(8,128)(2,1)S(1)} %bitcast.17), slice={[0:27], [0:240], [0:128]} | slice | bytes 3317760 | tf_op jit(solution)/shard_map/reshape | solution.py:323
  6.1 0.0 copy-done.1
  6.1 0.1 copy.9
  6.2 0.0 copy-start
  6.2 0.6 broadcast_in_dim.30
  6.9 0.1 copy.11
  7.0 0.2 broadcast_multiply_fusion.1
  7.1 0.7 copy.14
  7.9 0.0 copy-start.3
  7.9 0.2 broadcast_multiply_fusion
  8.1 1.4 %mul.64.bd_ref = bf16[320,320]{1,0:T(8,128)(2,1)} reshape(bf16[10,32,10,32]{3,2,1,0:T(8,128)(2,1)S(1)} %broadcast_multiply_fusion) | data formatting | bytes 409600 | tf_op jit(solution)/shard_map/jit(kron)/mul | solution.py:277
  9.5 0.0 copy-done
  9.5 0.0 copy-done.3
  9.5 0.0 copy-done.2
  9.5 0.1 broadcast_in_dim.33
  9.6 0.1 tile.10
  9.7 0.1 tile.12
  9.8 0.6 pad.4.id_ref
  10.4 106.6 %apply_all.1 = bf16[16,4096]{1,0:T(8,128)(2,1)} custom-call(s32[32]{0:T(128)} %bitcast.29, s32[16]{0:T(128)} %reshape.57.kind_ref, bf16[32,16,256]{2,1,0:T(8,128)(2,1)} %bitcast.19, bf16[27,240,128]{2,1,0:T(8,128)(2,1)} %slice.tab_ref, bf16[32,32]{1,0:T(8,128)(2,1)} %w_ref.1, bf16[32,32]{1,0:T(8,128)(2,1)} %bitcast.26, bf16[64,32]{1,0:T(8,128)(2,1)} %bitcast.27, ...), custom_call_target="tpu_custom_call" | custom-call | tf_op jit(solution)/shard_map/apply_all/pallas_call | solution.py:278
  117.0 1.6 %copy.16 = bf16[16,1,4096]{2,0,1:T(8,128)(2,1)} copy(bf16[16,1,4096]{2,0,1:T(8,128)(2,1)} %bitcast.22) | data formatting | bytes 262144
  (9 shorter events, 0.1 us)
Async XLA Ops:
  4.8 1.3 %copy-start.1 = (bf16[32,32]{1,0:T(8,128)(2,1)S(1)}, bf16[32,32]{1,0:T(8,128)(2,1)}, u32[]{:S(2)}) copy-start(bf16[32,32]{1,0:T(8,128)(2,1)} %w_ref.1) | copy-start | bytes 6148
  6.2 3.3 %copy-start = (bf16[32,32]{0,1:T(8,128)(2,1)}, bf16[32,32]{0,1:T(8,128)(2,1)S(1)}, u32[]{:S(2)}) copy-start(bf16[32,32]{0,1:T(8,128)(2,1)S(1)} %copy.9) | copy-start | bytes 6148
  7.9 1.6 %copy-start.3 = (s32[4,4,1]{1,2,0:T(1,128)S(1)}, s32[4,4,1]{1,2,0:T(1,128)}, u32[]{:S(2)}) copy-start(s32[4,4,1]{1,2,0:T(1,128)} %param.12) | copy-start | bytes 196
  7.9 1.6 %copy-start.2 = (s32[4,4]{1,0:T(4,128)S(1)}, s32[4,4]{1,0:T(4,128)}, u32[]{:S(2)}) copy-start(s32[4,4]{1,0:T(4,128)} %param.13) | copy-start | bytes 196

commit v3 on v2

--- a/solution.py
+++ b/solution.py
@@ -22,21 +22,34 @@
     return lax.dot_general(a, b, dims, preferred_element_type=F32)
 
 
+def one_hot(hit):
+    return jnp.where(hit, 1.0, 0.0).astype(BF)
+
+
+def iotas(rows, cols):
+    return (
+        lax.broadcasted_iota(jnp.int32, (rows, cols), 0),
+        lax.broadcasted_iota(jnp.int32, (rows, cols), 1),
+    )
+
+
 def apply_all_kernel(
-    slot_ref, kind_ref, ch_ref, tab_ref, w_ref, wt_ref, wtd_ref, wc4_ref, bd_ref, id_ref, out_ref,
-    stage, blocks, mask2, mask3, flat, h0s, base2, base3, s1, lhs3, e3, totals, pieces,
-    rows, idx, idy, select, acc, part, from_low, from_high,
+    slot_ref, kind_ref, leaf_ref, node_ref, ch_ref, tab_ref, w_ref, out_ref,
+    stage, blocks, mask2, mask3, wt, wtd, wc4, bd, flat, h0s, base2, base3, s1, lhs3, e3,
+    totals, pieces, rows, idx, idy, select, acc, part, from_low, from_high,
     es, er, xs, xr, ixs, ixr, ys, yr, fs, fr, iys, iyr, ps, pr, ms, mr,
 ):
     leaf, octant = lax.axis_index("leaf"), lax.axis_index("oct")
     z, y = leaf // NY, lax.rem(leaf, NY)
+    chip, core = octant // 2, lax.rem(octant, 2)
 
     def at_y(d):
         return (z * NY + lax.rem(y + d, NY), octant)
 
     up_z = (lax.rem(z + 1, NZ) * NY + y, octant)
     down_z = (lax.rem(z + NZ - 1, NZ) * NY + y, octant)
-    targets = [lax.rem(octant + d, NO) for d in range(NO)]
+    hops = [(2, 0), (2, 1), (1, 0), (1, 1), (3, 0), (3, 1), (0, 1)]
+    target = {(e, c): lax.rem(chip + e, 4) * 2 + lax.rem(core + c, 2) for e, c in hops}
 
     def remote(src, dst, ss, rs, where):
         copy = pltpu.make_async_remote_copy(
@@ -47,78 +60,108 @@
         return copy
 
     barrier = pltpu.get_barrier_semaphore()
-    partners = [(leaf, targets[d]) for d in range(1, NO)]
+    partners = [(leaf, target[hop]) for hop in hops]
     partners += [at_y(1), at_y(2), at_y(3), up_z, down_z]
     for partner in partners:
         pl.semaphore_signal(barrier, inc=1, device_id=partner, device_id_type=MESH)
     for q in range(32):
-        stage[q // 4, q % 4] = ch_ref[slot_ref[q]]
-    idx[octant] = id_ref[...]
+        stage[q // 4, q % 4] = ch_ref[slot_ref[q, 0]]
+    row, col = iotas(8, 128)
+    goal = jnp.zeros((8, 128), jnp.int32)
+    for p in range(NP):
+        for k in range(4):
+            goal = jnp.where(
+                (row == p) & (col % 16 // 4 == k), leaf_ref[p, k] * 16 + node_ref[p, k], goal
+            )
+    idx[octant] = jnp.where(col // 16 == octant, goal, 0)
     pl.semaphore_wait(barrier, len(partners))
 
     e_copies, ix_copies = [], []
-    for d in range(1, NO):
-        where = (leaf, targets[d])
+    for e, c in hops:
+        to = target[e, c]
         e_copies.append(
-            remote(stage.at[targets[d]], blocks.at[octant], es.at[d], er.at[d], where)
+            remote(stage.at[to], blocks.at[octant], es.at[e, c], er.at[e, c], (leaf, to))
         )
-    for d in range(1, NO):
-        where = (leaf, targets[d])
-        ix_copies.append(remote(id_ref, idx.at[octant], ixs.at[d], ixr.at[d], where))
+    for e, c in hops:
+        to = target[e, c]
+        ix_copies.append(
+            remote(idx.at[octant], idx.at[octant], ixs.at[e, c], ixr.at[e, c], (leaf, to))
+        )
     blocks[octant] = stage[octant]
 
-    row = lax.broadcasted_iota(jnp.int32, (256, 256), 0)
-    col = lax.broadcasted_iota(jnp.int32, (256, 256), 1)
-    mask2[...] = jnp.where(col % 8 == (row // 16) % 8, 1.0, 0.0).astype(BF)
-    mask3[...] = jnp.where(col % 8 == (row // 8) % 8, 1.0, 0.0).astype(BF)
-
-    def fold(n, carry):
-        dense = tab_ref[kind_ref[n]].astype(F32)
+    w = w_ref[...]
+    row, col = iotas(256, 256)
+    mask2[...] = one_hot(col % 8 == (row // 16) % 8)
+    mask3[...] = one_hot(col % 8 == (row // 8) % 8)
+    row, col = iotas(32, 32)
+    wt[...] = mm(one_hot(row == col), w, NT).astype(BF)
+    row, col = iotas(64, 32)
+    wtd[...] = mm(one_hot(col == row // 16 * 8 + row % 8), w, NT).astype(BF)
+    row, col = iotas(320, 32)
+    tile = one_hot(row % 32 == col)
+    row, col = iotas(32, 1024)
+    wide = mm(w, one_hot(col % 256 // 8 == row)).astype(BF)
+    row, col = iotas(128, 1024)
+    wc4[...] = jnp.where(row // 32 == col // 256, mm(tile[0:128], wide), 0.0).astype(BF)
+    row, col = iotas(320, 320)
+    tall = mm(tile, w, NT).astype(BF)
+    bd[...] = jnp.where(row // 32 == col // 32, mm(tall, tile, NT), 0.0).astype(BF)
+
+    def fold(p, k):
+        n = p * 4 + k
+        dense = tab_ref[kind_ref[p, k]].astype(F32)
         for o in range(4):
             flat[pl.ds(o, 240, stride=4), :] = dense[:, o * 32:(o + 1) * 32]
         g0 = mm(flat[0:320, :].astype(BF), w_ref[...]).astype(BF)
-        h0s[n] = mm(bd_ref[...], g0).astype(BF)
-        a1 = mm(wtd_ref[...], flat[320:640, :].astype(BF), NT).astype(BF)
-        a2 = mm(wt_ref[...], flat[640:960, :].astype(BF), NT).astype(BF)
+        h0s[n] = mm(bd[...], g0).astype(BF)
+        a1 = mm(wtd[...], flat[320:640, :].astype(BF), NT).astype(BF)
+        a2 = mm(wt[...], flat[640:960, :].astype(BF), NT).astype(BF)
         for g, width in ((0, 128), (1, 128), (2, 64)):
             ins = slice(g * 128, g * 128 + width)
             outs = slice(g * 1024, g * 1024 + width * 8)
-            base3[n, :, outs] = mm(a1[:, ins], wc4_ref[0:width, 0:width * 8]).astype(BF)
-            base2[n, :, outs] = mm(a2[:, ins], wc4_ref[0:width, 0:width * 8]).astype(BF)
+            base3[n, :, outs] = mm(a1[:, ins], wc4[0:width, 0:width * 8]).astype(BF)
+            base2[n, :, outs] = mm(a2[:, ins], wc4[0:width, 0:width * 8]).astype(BF)
+
+    def fold_first(k, carry):
+        fold(0, k)
         return carry
 
-    lax.fori_loop(0, 16, fold, 0)
+    lax.fori_loop(0, 4, fold_first, 0)
     for copy in e_copies:
         copy.wait()
 
     x_copies, y_copies, f_copies = {}, {}, {}
 
     def send_x(p):
-        for d in range(1, NO):
-            x_copies[p, d] = remote(
-                pieces.at[p, targets[d]], rows.at[y, p, octant], xs.at[p, d], xr.at[p, d],
-                (leaf, targets[d]),
+        rows[y, p, octant] = pieces[p, octant]
+        for e, c in hops:
+            to = target[e, c]
+            x_copies[p, e, c] = remote(
+                pieces.at[p, to], rows.at[y, p, octant], xs.at[p, e, c], xr.at[p, e, c],
+                (leaf, to),
             )
-        rows[y, p, octant] = pieces[p, octant]
-
-    def send_y(p):
-        for d in range(1, NO):
-            x_copies[p, d].wait_recv()
-        block = rows.at[y, p]
-        y_copies[p] = (
-            remote(block, block, ys.at[0, p], yr.at[0, p], at_y(1)),
-            remote(block, block, ys.at[1, p], yr.at[1, p], at_y(3)),
+
+    def pair_of(e):
+        return pl.ds(lax.rem(chip + 4 - e, 4) * 2, 2)
+
+    def send_y(p, e):
+        for c in range(2):
+            if (e, c) != (0, 0):
+                x_copies[p, e, c].wait_recv()
+        block = rows.at[y, p, pair_of(e)]
+        y_copies[p, e] = (
+            remote(block, block, ys.at[0, p, e], yr.at[0, p, e], at_y(1)),
+            remote(block, block, ys.at[1, p, e], yr.at[1, p, e], at_y(3)),
         )
 
-    def forward(p):
-        up, down = y_copies[p]
-        up.wait_recv()
-        block = rows.at[lax.rem(y + NY - 1, NY), p, 0:4]
-        first = remote(block, block, fs.at[0, p], fr.at[0, p], at_y(1))
-        down.wait_recv()
-        block = rows.at[lax.rem(y + 1, NY), p, 4:8]
-        second = remote(block, block, fs.at[1, p], fr.at[1, p], at_y(3))
-        f_copies[p] = (first, second)
+    def forward(p, *which):
+        for e in which:
+            up, down = y_copies[p, e]
+            up.wait_recv()
+            down.wait_recv()
+            came, to = (NY - 1, 1) if e < 2 else (1, 3)
+            block = rows.at[lax.rem(y + came, NY), p, pair_of(e)]
+            f_copies[p, e] = remote(block, block, fs.at[p, e], fr.at[p, e], at_y(to))
 
     iy_copies = []
     for p in range(NP):
@@ -163,24 +206,33 @@
                             totals[4 * i + 2 * j + l, pl.ds(start, 16), :] = total[
                                 r:r + 16, j * 128:(j + 1) * 128
                             ]
+            if p < NP - 1:
+                fold(p + 1, k)
             return carry
 
-        lax.fori_loop(0, 3, entry, 0)
+        lax.fori_loop(0, 2, entry, 0)
         if p == 0:
             for copy in ix_copies:
                 copy.wait()
             idy[y] = jnp.sum(idx[...], axis=0)
             for d in range(1, NY):
                 iy_copies.append(remote(idy.at[y], idy.at[y], iys.at[d], iyr.at[d], at_y(d)))
-        if p >= 1:
-            send_y(p - 1)
-        lax.fori_loop(3, 4, entry, 0)
+        else:
+            send_y(p - 1, 0)
+        if p >= 2:
+            send_y(p - 2, 2)
+        if p >= 3:
+            forward(p - 3, 2)
+        lax.fori_loop(2, 4, entry, 0)
         for o in range(NO):
             for r in range(8):
                 pieces[p, o, r] = totals[o, pl.ds(r, 16, stride=8), :].astype(BF)
         send_x(p)
+        if p >= 1:
+            send_y(p - 1, 1)
+            send_y(p - 1, 3)
         if p >= 2:
-            forward(p - 2)
+            forward(p - 2, 0, 1, 3)
 
     rho = lax.broadcasted_iota(jnp.int32, (256, 128), 0)
     key = (rho // 16) * 64 + y * 16 + rho % 16
@@ -191,8 +243,8 @@
             for s in range(NY):
                 hit = (key == idy[s, p:p + 1, :]) & (lane % 4 == h)
                 select[h, :, s * 128:(s + 1) * 128] = jnp.where(hit, 1.0, 0.0).astype(BF)
-        for copy in f_copies[p]:
-            copy.wait_recv()
+        for e in range(4):
+            f_copies[p, e].wait_recv()
 
         def two_rows(r, carry):
             lo = rows[:, p, :, 2 * r].reshape(512, 128)
@@ -214,11 +266,15 @@
 
     for copy in iy_copies:
         copy.wait()
+    send_y(3, 0)
+    send_y(2, 2)
     node_sums(0)
-    send_y(3)
-    forward(2)
+    for e in (1, 3, 2):
+        send_y(3, e)
+    forward(1, 2)
+    forward(2, 0, 1, 3, 2)
     node_sums(1)
-    forward(3)
+    forward(3, 0, 1, 3, 2)
     node_sums(2)
     node_sums(3)
 
@@ -242,8 +298,7 @@
                 down_copies[s, u] = remote(
                     part.at[low, span], from_high.at[s, span], ms.at[s, u], mr.at[s, u], down_z
                 )
-    row = lax.broadcasted_iota(jnp.int32, (256, 256), 0)
-    col = lax.broadcasted_iota(jnp.int32, (256, 256), 1)
+    row, col = iotas(256, 256)
     source_lane = (col % 16) // 8 * 128 + (col // 16) * 8 + col % 8
     perm = jnp.where(row == source_lane, 1.0, 0.0).astype(BF)
     for u in range(SUBS):
@@ -262,29 +317,31 @@
     for copy in list(up_copies.values()) + list(down_copies.values()):
         copy.wait_send()
     for p in range(NP):
-        for copy in f_copies[p] + y_copies[p]:
-            copy.wait_send()
-        for d in range(1, NO):
-            x_copies[p, d].wait_send()
-
-
-def apply_all(slots, kinds, child_cubes, table, two_scale, ids):
+        for e in range(4):
+            f_copies[p, e].wait_send()
+            for copy in y_copies[p, e]:
+                copy.wait_send()
+        for hop in hops:
+            x_copies[p, hop[0], hop[1]].wait_send()
+
+
+def apply_all(slots, kinds, leaves, nodes, child_cubes, table, two_scale):
     dma = pltpu.SemaphoreType.DMA
     smem = pl.BlockSpec(memory_space=pltpu.SMEM)
-    wt = two_scale.T
-    wtd = jnp.broadcast_to(wt.reshape(4, 1, 8, 32), (4, 2, 8, 32)).reshape(64, 32)
-    wc4 = jnp.kron(jnp.eye(4, dtype=BF), jnp.repeat(two_scale, 8, axis=1))
-    bd = jnp.kron(jnp.eye(10, dtype=BF), wt)
     return pl.pallas_call(
         apply_all_kernel,
         out_shape=jax.ShapeDtypeStruct((16, 4096), BF),
-        in_specs=[smem, smem] + [VM] * 8,
+        in_specs=[smem] * 4 + [VM] * 3,
         out_specs=VM,
         scratch_shapes=[
             pltpu.VMEM((NO, NP, 16, 256), BF),
             pltpu.VMEM((NO, NP, 16, 256), BF),
             pltpu.VMEM((256, 256), BF),
             pltpu.VMEM((256, 256), BF),
+            pltpu.VMEM((32, 32), BF),
+            pltpu.VMEM((64, 32), BF),
+            pltpu.VMEM((128, 1024), BF),
+            pltpu.VMEM((320, 320), BF),
             pltpu.VMEM((960, 32), F32),
             pltpu.VMEM((16, 320, 32), BF),
             pltpu.VMEM((16, 32, 2560), BF),
@@ -302,25 +359,21 @@
             pltpu.VMEM((NZ, 32, 16, 128), BF),
             pltpu.VMEM((8, 32, 16, 128), BF),
             pltpu.VMEM((7, 32, 16, 128), BF),
-            dma((NO,)), dma((NO,)), dma((NP, NO)), dma((NP, NO)), dma((NO,)), dma((NO,)),
-            dma((2, NP)), dma((2, NP)), dma((2, NP)), dma((2, NP)), dma((NY,)), dma((NY,)),
+            dma((4, 2)), dma((4, 2)), dma((NP, 4, 2)), dma((NP, 4, 2)), dma((4, 2)), dma((4, 2)),
+            dma((2, NP, 4)), dma((2, NP, 4)), dma((NP, 4)), dma((NP, 4)), dma((NY,)), dma((NY,)),
             dma((8, SUBS)), dma((8, SUBS)), dma((7, SUBS)), dma((7, SUBS)),
         ],
         compiler_params=pltpu.CompilerParams(
             collective_id=0, has_side_effects=True, vmem_limit_bytes=56 << 20
         ),
         name="apply_all",
-    )(slots, kinds, child_cubes, table, two_scale, wt, wtd, wc4, bd, ids)
+    )(slots, kinds, leaves, nodes, child_cubes, table, two_scale)
 
 
 def local(children, child_slot, two_scale, factors, disp_kind, target_leaf, target_node):
-    goal = (target_leaf[:, :, 0] * 16 + target_node).astype(jnp.int32)
-    lane = jnp.arange(128, dtype=jnp.int32)
-    spread = jnp.tile(jnp.repeat(goal, 4, axis=1), (1, NO))
-    ids = jnp.where(lane // 16 == lax.axis_index("oct"), spread, 0)
     out = apply_all(
-        child_slot.reshape(-1), disp_kind.reshape(-1), children.reshape(32, 16, 256),
-        factors.reshape(-1, 240, 128), two_scale, jnp.pad(ids, ((0, 4), (0, 0))),
+        child_slot, disp_kind, target_leaf[:, :, 0], target_node,
+        children.reshape(32, 16, 256), factors.reshape(-1, 240, 128), two_scale,
     )
     return out.reshape(16, 1, 4096)
 

time: 119 us -> 106 us (0.89)
  Pallas kernels: 107 us -> 99.7 us
  local copies, waits for them, and re-layouts: 11.5 us -> 6.1 us
    pallas_call x1, Pallas kernels: 107 us -> 99.7 us  [apply_all(): pl.pallas_call(apply_all_kernel, out_shape=jax.ShapeDtypeStruct((16, 4096...]
    mul x3 -> x0, local copies, waits for them, and re-layouts: 1.52 us -> none  [the longest x1 1.44 us: apply_all(): bd = jnp.kron(jnp.eye(10, dtype=BF), wt)]
    reshape x1 -> x0, local copies, waits for them, and re-layouts: 1.33 us -> none  [local(): disp_kind.reshape(-1)]
    unnamed x13 -> x8, local copies, waits for them, and re-layouts: 5.91 us -> 4.82 us
where the time goes in v3:
time: 106 us
  Pallas kernels  99.7 us (94%)
  local copies, waits for them, and re-layouts  6.1 us (6%)
    pallas_call x1, Pallas kernels, apply_all(): pl.pallas_call(apply_all_kernel, out_shape=jax.ShapeDtypeStruct((16, 4096...  99.7 us
    unnamed x8, local copies, waits for them, and re-layouts  4.82 us

profile of v3, /device:TPU:2, one launch (start us, length us, event | category | flops | bytes accessed | tf_op | source)
XLA Modules:
  0.0 105.8 jit_solution(10167058622885305648)
XLA Ops:
  0.0 1.8 %copy.10 = bf16[4,8,240,128]{3,2,1,0:T(8,128)(2,1)S(1)} copy(bf16[4,8,240,128]{3,1,2,0:T(8,128)(2,1)} %bitcast.8) | data formatting | bytes 3932160
  1.8 0.0 copy-start
  1.8 0.0 copy-start.1
  1.8 1.3 %slice.tab_ref = bf16[27,240,128]{2,1,0:T(8,128)(2,1)} slice(bf16[32,240,128]{2,1,0:T(8,128)(2,1)S(1)} %bitcast.7), slice={[0:27], [0:240], [0:128]} | slice | bytes 3317760 | tf_op jit(solution)/shard_map/reshape | solution.py:376
  3.1 0.0 copy-done
  3.1 0.7 copy.9
  3.9 0.0 copy-done.1
  3.9 0.7 copy.8.slot_ref
  4.6 99.7 %apply_all.1 = bf16[16,4096]{1,0:T(8,128)(2,1)} custom-call(s32[32,1]{1,0:T(8,128)} %copy.8.slot_ref, s32[4,4]{1,0:T(4,128)} %kind_ref.1, s32[4,4]{1,0:T(4,128)} %bitcast.12, s32[4,4]{1,0:T(4,128)} %node_ref.1, bf16[32,16,256]{2,1,0:T(8,128)(2,1)} %bitcast.9, bf16[27,240,128]{2,1,0:T(8,128)(2,1)} %slice.tab_ref, bf16[32,32]{1,0:T(8,128)(2,1)} %w_ref.1), custom_call_target="tpu_custom_call" | custom-call | tf_op jit(solution)/shard_map/apply_all/pallas_call | solution.py:331
  104.3 1.6 %copy.12 = bf16[16,1,4096]{2,0,1:T(8,128)(2,1)} copy(bf16[16,1,4096]{2,0,1:T(8,128)(2,1)} %bitcast.10) | data formatting | bytes 262144
Async XLA Ops:
  1.8 1.3 %copy-start = (bf16[32,4096]{1,0:T(8,128)(2,1)S(1)}, bf16[32,4096]{1,0:T(8,128)(2,1)}, u32[]{:S(2)}) copy-start(bf16[32,4096]{1,0:T(8,128)(2,1)} %param.7) | copy-start | bytes 786436
  1.8 2.0 %copy-start.1 = (s32[32,1]{0,1:T(1,128)S(1)}, s32[32,1]{0,1:T(1,128)}, u32[]{:S(2)}) copy-start(s32[32,1]{0,1:T(1,128)} %param.8) | copy-start | bytes 388

commit v4 on v3

--- a/solution.py
+++ b/solution.py
@@ -14,7 +14,7 @@
 NT = (((1,), (1,)), ((), ()))
 NN = (((1,), (0,)), ((), ()))
 NY, NZ, NO = 4, 16, 8
-SUBS = 4
+SUBS = 2
 NP = 4
 
 
@@ -144,24 +144,30 @@
     def pair_of(e):
         return pl.ds(lax.rem(chip + 4 - e, 4) * 2, 2)
 
-    def send_y(p, e):
-        for c in range(2):
-            if (e, c) != (0, 0):
-                x_copies[p, e, c].wait_recv()
-        block = rows.at[y, p, pair_of(e)]
-        y_copies[p, e] = (
-            remote(block, block, ys.at[0, p, e], yr.at[0, p, e], at_y(1)),
-            remote(block, block, ys.at[1, p, e], yr.at[1, p, e], at_y(3)),
-        )
-
-    def forward(p, *which):
+    def rows_of(p, half):
+        return pl.ds(0, 8) if p < 2 else pl.ds(half * 4, 4)
+
+    def send_y(p, half, *which):
         for e in which:
-            up, down = y_copies[p, e]
+            for c in range(2):
+                if half == 0 and (e, c) != (0, 0):
+                    x_copies[p, e, c].wait_recv()
+            block = rows.at[y, p, pair_of(e), rows_of(p, half)]
+            y_copies[p, e, half] = (
+                remote(block, block, ys.at[0, half, p, e], yr.at[0, half, p, e], at_y(1)),
+                remote(block, block, ys.at[1, half, p, e], yr.at[1, half, p, e], at_y(3)),
+            )
+
+    def forward(p, half, *which):
+        for e in which:
+            up, down = y_copies[p, e, half]
             up.wait_recv()
             down.wait_recv()
             came, to = (NY - 1, 1) if e < 2 else (1, 3)
-            block = rows.at[lax.rem(y + came, NY), p, pair_of(e)]
-            f_copies[p, e] = remote(block, block, fs.at[p, e], fr.at[p, e], at_y(to))
+            block = rows.at[lax.rem(y + came, NY), p, pair_of(e), rows_of(p, half)]
+            f_copies[p, e, half] = remote(
+                block, block, fs.at[half, p, e], fr.at[half, p, e], at_y(to)
+            )
 
     iy_copies = []
     for p in range(NP):
@@ -218,72 +224,63 @@
             for d in range(1, NY):
                 iy_copies.append(remote(idy.at[y], idy.at[y], iys.at[d], iyr.at[d], at_y(d)))
         else:
-            send_y(p - 1, 0)
+            send_y(p - 1, 0, 0)
         if p >= 2:
-            send_y(p - 2, 2)
+            send_y(p - 2, 0, 2)
         if p >= 3:
-            forward(p - 3, 2)
+            forward(p - 3, 0, 2)
         lax.fori_loop(2, 4, entry, 0)
         for o in range(NO):
             for r in range(8):
                 pieces[p, o, r] = totals[o, pl.ds(r, 16, stride=8), :].astype(BF)
         send_x(p)
         if p >= 1:
-            send_y(p - 1, 1)
-            send_y(p - 1, 3)
+            send_y(p - 1, 0, 1, 3)
         if p >= 2:
-            forward(p - 2, 0, 1, 3)
+            forward(p - 2, 0, 0, 1, 3)
 
     rho = lax.broadcasted_iota(jnp.int32, (256, 128), 0)
     key = (rho // 16) * 64 + y * 16 + rho % 16
     lane = lax.broadcasted_iota(jnp.int32, (256, 128), 1)
 
-    def node_sums(p):
-        for h in range(4):
-            for s in range(NY):
-                hit = (key == idy[s, p:p + 1, :]) & (lane % 4 == h)
-                select[h, :, s * 128:(s + 1) * 128] = jnp.where(hit, 1.0, 0.0).astype(BF)
+    def node_sums(p, half):
+        if half == 0:
+            for h in range(4):
+                for q in range(NY):
+                    hit = (key == idy[q, p:p + 1, :]) & (lane % 4 == h)
+                    select[p, h, :, q * 128:(q + 1) * 128] = one_hot(hit)
         for e in range(4):
-            f_copies[p, e].wait_recv()
+            f_copies[p, e, half].wait_recv()
 
         def two_rows(r, carry):
             lo = rows[:, p, :, 2 * r].reshape(512, 128)
             hi = rows[:, p, :, 2 * r + 1].reshape(512, 128)
             both = jnp.concatenate([lo, hi], axis=1)
             for h in range(4):
-                new = mm(select[h], both)
+                new = mm(select[p, h], both)
                 if p > 0:
                     new = new + acc[h, r]
                 if p < NP - 1:
                     acc[h, r] = new
                 else:
                     new = new.astype(BF)
-                    part[:, h * 8 + 2 * r] = new[:, 0:128].reshape(NZ, 16, 128)
-                    part[:, h * 8 + 2 * r + 1] = new[:, 128:256].reshape(NZ, 16, 128)
+                    at = half * 16 + h * 4 + 2 * (r - 2 * half)
+                    part[:, at] = new[:, 0:128].reshape(NZ, 16, 128)
+                    part[:, at + 1] = new[:, 128:256].reshape(NZ, 16, 128)
             return carry
 
-        lax.fori_loop(0, 4, two_rows, 0)
-
-    for copy in iy_copies:
-        copy.wait()
-    send_y(3, 0)
-    send_y(2, 2)
-    node_sums(0)
-    for e in (1, 3, 2):
-        send_y(3, e)
-    forward(1, 2)
-    forward(2, 0, 1, 3, 2)
-    node_sums(1)
-    forward(3, 0, 1, 3, 2)
-    node_sums(2)
-    node_sums(3)
-
-    width = 32 // SUBS
+        if p < 2:
+            lax.fori_loop(0, 4, two_rows, 0)
+        else:
+            lax.fori_loop(2 * half, 2 * half + 2, two_rows, 0)
+
+    width = 16 // SUBS
     up_copies, down_copies = {}, {}
-    for s in range(8):
+
+    def ring(s, half):
         high = lax.rem(z + 8 - s, NZ)
         low = lax.rem(z + NZ - 7 + s, NZ)
-        for u in range(SUBS):
+        for u in range(half * SUBS, (half + 1) * SUBS):
             span = pl.ds(u * width, width)
             if s > 0:
                 up_copies[s - 1, u].wait_recv()
@@ -298,29 +295,69 @@
                 down_copies[s, u] = remote(
                     part.at[low, span], from_high.at[s, span], ms.at[s, u], mr.at[s, u], down_z
                 )
+
     row, col = iotas(256, 256)
     source_lane = (col % 16) // 8 * 128 + (col // 16) * 8 + col % 8
-    perm = jnp.where(row == source_lane, 1.0, 0.0).astype(BF)
-    for u in range(SUBS):
-        down_copies[6, u].wait_recv()
-        up_copies[7, u].wait_recv()
-    for u in range(16):
-        pair = []
-        for wh in range(2):
-            r = wh * 16 + u
-            pair.append((
-                part[z, r].astype(F32) + from_low[7, r].astype(F32) + from_high[6, r].astype(F32)
-            ).astype(BF))
-        out_ref[:, u * 256:(u + 1) * 256] = mm(
-            jnp.concatenate(pair, axis=1), perm
-        ).astype(BF)
+    mask2[...] = one_hot(row == source_lane)
+
+    def finish(half):
+        for u in range(half * SUBS, (half + 1) * SUBS):
+            down_copies[6, u].wait_recv()
+            up_copies[7, u].wait_recv()
+        for u in range(16):
+            if u % 8 // 4 != half:
+                continue
+            pair = []
+            for wh in range(2):
+                r = half * 16 + (wh * 2 + u // 8) * 4 + u % 4
+                pair.append((
+                    part[z, r].astype(F32)
+                    + from_low[7, r].astype(F32)
+                    + from_high[6, r].astype(F32)
+                ).astype(BF))
+            out_ref[:, u * 256:(u + 1) * 256] = mm(
+                jnp.concatenate(pair, axis=1), mask2[...]
+            ).astype(BF)
+
+    for copy in iy_copies:
+        copy.wait()
+    send_y(2, 0, 2)
+    send_y(3, 0, 0)
+    node_sums(0, 0)
+    send_y(3, 0, 1, 3, 2)
+    forward(1, 0, 2)
+    forward(2, 0, 0, 1, 3, 2)
+    send_y(2, 1, 0, 1, 3, 2)
+    node_sums(1, 0)
+    forward(3, 0, 0, 1, 3, 2)
+    send_y(3, 1, 0, 1, 3, 2)
+    node_sums(2, 0)
+    forward(2, 1, 0, 1, 3, 2)
+    node_sums(3, 0)
+    ring(0, 0)
+    ring(1, 0)
+    forward(3, 1, 0, 1, 3, 2)
+    ring(2, 0)
+    node_sums(2, 1)
+    ring(3, 0)
+    node_sums(3, 1)
+    ring(0, 1)
+    for s in range(4, 8):
+        ring(s, 0)
+        ring(s - 3, 1)
+    ring(5, 1)
+    finish(0)
+    ring(6, 1)
+    ring(7, 1)
+    finish(1)
     for copy in list(up_copies.values()) + list(down_copies.values()):
         copy.wait_send()
     for p in range(NP):
         for e in range(4):
-            f_copies[p, e].wait_send()
-            for copy in y_copies[p, e]:
-                copy.wait_send()
+            for half in range(1 if p < 2 else 2):
+                f_copies[p, e, half].wait_send()
+                for copy in y_copies[p, e, half]:
+                    copy.wait_send()
         for hop in hops:
             x_copies[p, hop[0], hop[1]].wait_send()
 
@@ -354,14 +391,15 @@
             pltpu.VMEM((NY, NP, NO, 8, 16, 128), BF),
             pltpu.VMEM((NO, 8, 128), jnp.int32),
             pltpu.VMEM((NY, 8, 128), jnp.int32),
-            pltpu.VMEM((4, 256, 512), BF),
+            pltpu.VMEM((NP, 4, 256, 512), BF),
             pltpu.VMEM((4, 4, 256, 256), F32),
             pltpu.VMEM((NZ, 32, 16, 128), BF),
             pltpu.VMEM((8, 32, 16, 128), BF),
             pltpu.VMEM((7, 32, 16, 128), BF),
             dma((4, 2)), dma((4, 2)), dma((NP, 4, 2)), dma((NP, 4, 2)), dma((4, 2)), dma((4, 2)),
-            dma((2, NP, 4)), dma((2, NP, 4)), dma((NP, 4)), dma((NP, 4)), dma((NY,)), dma((NY,)),
-            dma((8, SUBS)), dma((8, SUBS)), dma((7, SUBS)), dma((7, SUBS)),
+            dma((2, 2, NP, 4)), dma((2, 2, NP, 4)), dma((2, NP, 4)), dma((2, NP, 4)),
+            dma((NY,)), dma((NY,)),
+            dma((8, 2 * SUBS)), dma((8, 2 * SUBS)), dma((7, 2 * SUBS)), dma((7, 2 * SUBS)),
         ],
         compiler_params=pltpu.CompilerParams(
             collective_id=0, has_side_effects=True, vmem_limit_bytes=56 << 20

time: 106 us -> 110 us (1.038)
  Pallas kernels: 99.7 us -> 104 us
    pallas_call x1, Pallas kernels: 99.7 us -> 104 us  [apply_all(): pl.pallas_call(apply_all_kernel, out_shape=jax.ShapeDtypeStruct((16, 4096...]
where the time goes in v4:
time: 110 us
  Pallas kernels  104 us (95%)
  local copies, waits for them, and re-layouts  6.1 us (6%)
    pallas_call x1, Pallas kernels, apply_all(): pl.pallas_call(apply_all_kernel, out_shape=jax.ShapeDtypeStruct((16, 4096...  104 us
    unnamed x8, local copies, waits for them, and re-layouts  4.82 us

profile of v4, /device:TPU:2, one launch (start us, length us, event | category | flops | bytes accessed | tf_op | source)
XLA Modules:
  0.0 109.8 jit_solution(2481483887688166062)
XLA Ops:
  0.0 1.8 %copy.10 = bf16[4,8,240,128]{3,2,1,0:T(8,128)(2,1)S(1)} copy(bf16[4,8,240,128]{3,1,2,0:T(8,128)(2,1)} %bitcast.8) | data formatting | bytes 3932160
  1.8 0.0 copy-start
  1.8 0.0 copy-start.1
  1.8 1.3 %slice.tab_ref = bf16[27,240,128]{2,1,0:T(8,128)(2,1)} slice(bf16[32,240,128]{2,1,0:T(8,128)(2,1)S(1)} %bitcast.7), slice={[0:27], [0:240], [0:128]} | slice | bytes 3317760 | tf_op jit(solution)/shard_map/reshape | solution.py:414
  3.1 0.0 copy-done
  3.1 0.7 copy.9
  3.9 0.0 copy-done.1
  3.9 0.7 copy.8.slot_ref
  4.6 103.7 %apply_all.1 = bf16[16,4096]{1,0:T(8,128)(2,1)} custom-call(s32[32,1]{1,0:T(8,128)} %copy.8.slot_ref, s32[4,4]{1,0:T(4,128)} %kind_ref.1, s32[4,4]{1,0:T(4,128)} %bitcast.12, s32[4,4]{1,0:T(4,128)} %node_ref.1, bf16[32,16,256]{2,1,0:T(8,128)(2,1)} %bitcast.9, bf16[27,240,128]{2,1,0:T(8,128)(2,1)} %slice.tab_ref, bf16[32,32]{1,0:T(8,128)(2,1)} %w_ref.1), custom_call_target="tpu_custom_call" | custom-call | tf_op jit(solution)/shard_map/apply_all/pallas_call | solution.py:368
  108.3 1.6 %copy.12 = bf16[16,1,4096]{2,0,1:T(8,128)(2,1)} copy(bf16[16,1,4096]{2,0,1:T(8,128)(2,1)} %bitcast.10) | data formatting | bytes 262144
Async XLA Ops:
  1.8 1.3 %copy-start = (bf16[32,4096]{1,0:T(8,128)(2,1)S(1)}, bf16[32,4096]{1,0:T(8,128)(2,1)}, u32[]{:S(2)}) copy-start(bf16[32,4096]{1,0:T(8,128)(2,1)} %param.7) | copy-start | bytes 786436
  1.8 2.0 %copy-start.1 = (s32[32,1]{0,1:T(1,128)S(1)}, s32[32,1]{0,1:T(1,128)}, u32[]{:S(2)}) copy-start(s32[32,1]{0,1:T(1,128)} %param.8) | copy-start | bytes 388

commit v5 on v3

--- a/solution.py
+++ b/solution.py
@@ -48,7 +48,7 @@
 
     up_z = (lax.rem(z + 1, NZ) * NY + y, octant)
     down_z = (lax.rem(z + NZ - 1, NZ) * NY + y, octant)
-    hops = [(2, 0), (2, 1), (1, 0), (1, 1), (3, 0), (3, 1), (0, 1)]
+    hops = [(0, 1), (1, 0), (1, 1), (3, 0), (3, 1), (2, 0), (2, 1)]
     target = {(e, c): lax.rem(chip + e, 4) * 2 + lax.rem(core + c, 2) for e, c in hops}
 
     def remote(src, dst, ss, rs, where):
@@ -65,7 +65,7 @@
     for partner in partners:
         pl.semaphore_signal(barrier, inc=1, device_id=partner, device_id_type=MESH)
     for q in range(32):
-        stage[q // 4, q % 4] = ch_ref[slot_ref[q, 0]]
+        stage[q // 4, q % 4] = ch_ref[slot_ref[q]]
     row, col = iotas(8, 128)
     goal = jnp.zeros((8, 128), jnp.int32)
     for p in range(NP):
@@ -109,7 +109,7 @@
 
     def fold(p, k):
         n = p * 4 + k
-        dense = tab_ref[kind_ref[p, k]].astype(F32)
+        dense = tab_ref[kind_ref[n // 4, n % 4]].astype(F32)
         for o in range(4):
             flat[pl.ds(o, 240, stride=4), :] = dense[:, o * 32:(o + 1) * 32]
         g0 = mm(flat[0:320, :].astype(BF), w_ref[...]).astype(BF)
@@ -126,7 +126,7 @@
         fold(0, k)
         return carry
 
-    lax.fori_loop(0, 4, fold_first, 0)
+    lax.fori_loop(0, 8, fold_first, 0)
     for copy in e_copies:
         copy.wait()
 
@@ -206,7 +206,7 @@
                             totals[4 * i + 2 * j + l, pl.ds(start, 16), :] = total[
                                 r:r + 16, j * 128:(j + 1) * 128
                             ]
-            if p < NP - 1:
+            if 0 < p < NP - 1:
                 fold(p + 1, k)
             return carry
 
@@ -246,11 +246,11 @@
         for e in range(4):
             f_copies[p, e].wait_recv()
 
-        def two_rows(r, carry):
+        def two_rows(hs, r):
             lo = rows[:, p, :, 2 * r].reshape(512, 128)
             hi = rows[:, p, :, 2 * r + 1].reshape(512, 128)
             both = jnp.concatenate([lo, hi], axis=1)
-            for h in range(4):
+            for h in hs:
                 new = mm(select[h], both)
                 if p > 0:
                     new = new + acc[h, r]
@@ -260,9 +260,42 @@
                     new = new.astype(BF)
                     part[:, h * 8 + 2 * r] = new[:, 0:128].reshape(NZ, 16, 128)
                     part[:, h * 8 + 2 * r + 1] = new[:, 128:256].reshape(NZ, 16, 128)
+
+        def all_h(r, carry):
+            two_rows(range(4), r)
             return carry
 
-        lax.fori_loop(0, 4, two_rows, 0)
+        if p < NP - 1:
+            lax.fori_loop(0, 4, all_h, 0)
+        else:
+            for h in range(4):
+                for r in range(4):
+                    two_rows((h,), r)
+                if h < 2:
+                    ring_up(0, h)
+                else:
+                    ring_down(0, h)
+
+    width = 32 // SUBS
+    up_copies, down_copies = {}, {}
+
+    def ring_up(s, u):
+        to, span = lax.rem(z + 8 - s, NZ), pl.ds(u * width, width)
+        if (s - 1, u) in up_copies:
+            up_copies[s - 1, u].wait_recv()
+            part[to, span] = part[to, span] + from_low[s - 1, span]
+        up_copies[s, u] = remote(
+            part.at[to, span], from_low.at[s, span], ps.at[s, u], pr.at[s, u], up_z
+        )
+
+    def ring_down(s, u):
+        to, span = lax.rem(z + NZ - 8 + s, NZ), pl.ds(u * width, width)
+        if (s - 1, u) in down_copies:
+            down_copies[s - 1, u].wait_recv()
+            part[to, span] = part[to, span] + from_high[s - 1, span]
+        down_copies[s, u] = remote(
+            part.at[to, span], from_high.at[s, span], ms.at[s, u], mr.at[s, u], down_z
+        )
 
     for copy in iy_copies:
         copy.wait()
@@ -278,38 +311,22 @@
     node_sums(2)
     node_sums(3)
 
-    width = 32 // SUBS
-    up_copies, down_copies = {}, {}
-    for s in range(8):
-        high = lax.rem(z + 8 - s, NZ)
-        low = lax.rem(z + NZ - 7 + s, NZ)
+    for s in range(1, 8):
         for u in range(SUBS):
-            span = pl.ds(u * width, width)
-            if s > 0:
-                up_copies[s - 1, u].wait_recv()
-                part[high, span] = part[high, span] + from_low[s - 1, span]
-            up_copies[s, u] = remote(
-                part.at[high, span], from_low.at[s, span], ps.at[s, u], pr.at[s, u], up_z
-            )
-            if s < 7:
-                if s > 0:
-                    down_copies[s - 1, u].wait_recv()
-                    part[low, span] = part[low, span] + from_high[s - 1, span]
-                down_copies[s, u] = remote(
-                    part.at[low, span], from_high.at[s, span], ms.at[s, u], mr.at[s, u], down_z
-                )
+            ring_up(s, u)
+            ring_down(s, u)
     row, col = iotas(256, 256)
     source_lane = (col % 16) // 8 * 128 + (col // 16) * 8 + col % 8
     perm = jnp.where(row == source_lane, 1.0, 0.0).astype(BF)
     for u in range(SUBS):
-        down_copies[6, u].wait_recv()
+        down_copies[7, u].wait_recv()
         up_copies[7, u].wait_recv()
     for u in range(16):
         pair = []
         for wh in range(2):
             r = wh * 16 + u
             pair.append((
-                part[z, r].astype(F32) + from_low[7, r].astype(F32) + from_high[6, r].astype(F32)
+                part[z, r].astype(F32) + from_low[7, r].astype(F32) + from_high[7, r].astype(F32)
             ).astype(BF))
         out_ref[:, u * 256:(u + 1) * 256] = mm(
             jnp.concatenate(pair, axis=1), perm
@@ -358,10 +375,10 @@
             pltpu.VMEM((4, 4, 256, 256), F32),
             pltpu.VMEM((NZ, 32, 16, 128), BF),
             pltpu.VMEM((8, 32, 16, 128), BF),
-            pltpu.VMEM((7, 32, 16, 128), BF),
+            pltpu.VMEM((8, 32, 16, 128), BF),
             dma((4, 2)), dma((4, 2)), dma((NP, 4, 2)), dma((NP, 4, 2)), dma((4, 2)), dma((4, 2)),
             dma((2, NP, 4)), dma((2, NP, 4)), dma((NP, 4)), dma((NP, 4)), dma((NY,)), dma((NY,)),
-            dma((8, SUBS)), dma((8, SUBS)), dma((7, SUBS)), dma((7, SUBS)),
+            dma((8, SUBS)), dma((8, SUBS)), dma((8, SUBS)), dma((8, SUBS)),
         ],
         compiler_params=pltpu.CompilerParams(
             collective_id=0, has_side_effects=True, vmem_limit_bytes=56 << 20
@@ -372,7 +389,7 @@
 
 def local(children, child_slot, two_scale, factors, disp_kind, target_leaf, target_node):
     out = apply_all(
-        child_slot, disp_kind, target_leaf[:, :, 0], target_node,
+        child_slot.reshape(-1), disp_kind, target_leaf[:, :, 0], target_node,
         children.reshape(32, 16, 256), factors.reshape(-1, 240, 128), two_scale,
     )
     return out.reshape(16, 1, 4096)

time: 106 us -> 105 us (level)
  the two profiles are of different devices: /device:TPU:2 before, /device:TPU:32 now
where the time goes in v5:
time: 105 us; the launch traced here: 104 us
  Pallas kernels  99 us (94%)
  local copies, waits for them, and re-layouts  5.42 us (5%)
    pallas_call x1, Pallas kernels, apply_all(): pl.pallas_call(apply_all_kernel, out_shape=jax.ShapeDtypeStruct((16, 4096...  99 us
    unnamed x5, local copies, waits for them, and re-layouts  4.12 us

profile of v5, /device:TPU:32, one launch (start us, length us, event | category | flops | bytes accessed | tf_op | source)
XLA Modules:
  0.0 104.4 jit_solution(7184329018360189512)
XLA Ops:
  0.0 1.8 %copy.9 = bf16[4,8,240,128]{3,2,1,0:T(8,128)(2,1)S(1)} copy(bf16[4,8,240,128]{3,1,2,0:T(8,128)(2,1)} %bitcast.9) | data formatting | bytes 3932160
  1.8 0.0 copy-start
  1.8 1.3 %slice.tab_ref = bf16[27,240,128]{2,1,0:T(8,128)(2,1)} slice(bf16[32,240,128]{2,1,0:T(8,128)(2,1)S(1)} %bitcast.8), slice={[0:27], [0:240], [0:128]} | slice | bytes 3317760 | tf_op jit(solution)/shard_map/reshape | solution.py:393
  3.1 0.0 copy-done
  3.1 0.7 copy.8
  3.9 99.0 %apply_all.1 = bf16[16,4096]{1,0:T(8,128)(2,1)} custom-call(s32[32]{0:T(128)} %bitcast.14, s32[4,4]{1,0:T(4,128)} %kind_ref.1, s32[4,4]{1,0:T(4,128)} %bitcast.13, s32[4,4]{1,0:T(4,128)} %node_ref.1, bf16[32,16,256]{2,1,0:T(8,128)(2,1)} %bitcast.10, bf16[27,240,128]{2,1,0:T(8,128)(2,1)} %slice.tab_ref, bf16[32,32]{1,0:T(8,128)(2,1)} %w_ref.1), custom_call_target="tpu_custom_call" | custom-call | tf_op jit(solution)/shard_map/apply_all/pallas_call | solution.py:348
  102.9 1.6 %copy.11 = bf16[16,1,4096]{2,0,1:T(8,128)(2,1)} copy(bf16[16,1,4096]{2,0,1:T(8,128)(2,1)} %bitcast.11) | data formatting | bytes 262144
Async XLA Ops:
  1.8 1.3 %copy-start = (bf16[32,4096]{1,0:T(8,128)(2,1)S(1)}, bf16[32,4096]{1,0:T(8,128)(2,1)}, u32[]{:S(2)}) copy-start(bf16[32,4096]{1,0:T(8,128)(2,1)} %param.7) | copy-start | bytes 786436

commit v6 on v5

--- a/solution.py
+++ b/solution.py
@@ -157,8 +157,7 @@
     def forward(p, *which):
         for e in which:
             up, down = y_copies[p, e]
-            up.wait_recv()
-            down.wait_recv()
+            (up if e < 2 else down).wait_recv()
             came, to = (NY - 1, 1) if e < 2 else (1, 3)
             block = rows.at[lax.rem(y + came, NY), p, pair_of(e)]
             f_copies[p, e] = remote(block, block, fs.at[p, e], fr.at[p, e], at_y(to))
@@ -244,6 +243,7 @@
                 hit = (key == idy[s, p:p + 1, :]) & (lane % 4 == h)
                 select[h, :, s * 128:(s + 1) * 128] = jnp.where(hit, 1.0, 0.0).astype(BF)
         for e in range(4):
+            y_copies[p, e][1 if e < 2 else 0].wait_recv()
             f_copies[p, e].wait_recv()
 
         def two_rows(hs, r):

time: 105 us -> 105 us (level)
  no operation moved by 1% of the time
where the time goes in v6:
time: 105 us; the launch traced here: 104 us
  Pallas kernels  99 us (94%)
  local copies, waits for them, and re-layouts  5.42 us (5%)
    pallas_call x1, Pallas kernels, apply_all(): pl.pallas_call(apply_all_kernel, out_shape=jax.ShapeDtypeStruct((16, 4096...  99 us
    unnamed x5, local copies, waits for them, and re-layouts  4.12 us

profile of v6, /device:TPU:32, one launch (start us, length us, event | category | flops | bytes accessed | tf_op | source)
XLA Modules:
  0.0 104.4 jit_solution(16854787287678820323)
XLA Ops:
  0.0 1.8 %copy.9 = bf16[4,8,240,128]{3,2,1,0:T(8,128)(2,1)S(1)} copy(bf16[4,8,240,128]{3,1,2,0:T(8,128)(2,1)} %bitcast.9) | data formatting | bytes 3932160
  1.8 0.0 copy-start
  1.8 1.3 %slice.tab_ref = bf16[27,240,128]{2,1,0:T(8,128)(2,1)} slice(bf16[32,240,128]{2,1,0:T(8,128)(2,1)S(1)} %bitcast.8), slice={[0:27], [0:240], [0:128]} | slice | bytes 3317760 | tf_op jit(solution)/shard_map/reshape | solution.py:393
  3.1 0.0 copy-done
  3.1 0.7 copy.8
  3.9 99.0 %apply_all.1 = bf16[16,4096]{1,0:T(8,128)(2,1)} custom-call(s32[32]{0:T(128)} %bitcast.14, s32[4,4]{1,0:T(4,128)} %kind_ref.1, s32[4,4]{1,0:T(4,128)} %bitcast.13, s32[4,4]{1,0:T(4,128)} %node_ref.1, bf16[32,16,256]{2,1,0:T(8,128)(2,1)} %bitcast.10, bf16[27,240,128]{2,1,0:T(8,128)(2,1)} %slice.tab_ref, bf16[32,32]{1,0:T(8,128)(2,1)} %w_ref.1), custom_call_target="tpu_custom_call" | custom-call | tf_op jit(solution)/shard_map/apply_all/pallas_call | solution.py:348
  102.9 1.6 %copy.11 = bf16[16,1,4096]{2,0,1:T(8,128)(2,1)} copy(bf16[16,1,4096]{2,0,1:T(8,128)(2,1)} %bitcast.11) | data formatting | bytes 262144
Async XLA Ops:
  1.8 1.3 %copy-start = (bf16[32,4096]{1,0:T(8,128)(2,1)S(1)}, bf16[32,4096]{1,0:T(8,128)(2,1)}, u32[]{:S(2)}) copy-start(bf16[32,4096]{1,0:T(8,128)(2,1)} %param.7) | copy-start | bytes 786436
